TPU v7x, 32 devices: a whole 2x2x4 slice. The times are simulated.
32 devices in a mesh: dom: 32 (over z, y, x, core).
Axes of the slice: x: 2, y: 2, z: 4, core: 2. Of those that a mesh axis runs over, the one named last changes fastest.
Arguments:
- coef_init: float32 [1024, 128], P('dom'), may hold values from -6 to 6
- basis: bfloat16 [49152, 1024], P('dom'), may hold values from -0.375 to 0.375
- basis_scale: float32 [384], P('dom'), may hold values from 0.5 to 2
- ext_force: float32 [49152, 128], P('dom'), may hold values from -6 to 6
- precond: float32 [1024], P('dom'), may hold values from 0.5 to 6, as said below
- connectivity: int32 [14400, 8], P('dom'), may hold values from 0 to 767, as said below
- halo_nodes: int32 [8192], P('dom'), may hold values from 0 to 511, as said below
- plastic: int32 [14400], P('dom'), may hold values 0 or 1
Outputs:
- coef_final: float32 [1024, 128], P('dom')
- nodal_residual: float32 [49152, 128], P('dom')
Inputs may be any that keep to these rules, and one draw needn't show every extreme that they name: `connectivity`: each part is a structured block of 16 x 16 x 2 nodes, numbered in a part-specific order; each row lists an element's 8 corners in corner-bit order (bit 0 along x, bit 1 along y, bit 2 along z). Entries below 512 are the part's own nodes; an entry 512 + h names the node listed h-th in the next part's halo_nodes (the next part's first z layer). `halo_nodes`: the entries of one part are its own local node numbers of its first z layer, in grid order with x fastest, all distinct. `precond`: Positive.
All inputs are finite; a program needn't handle non-finite values. No bound on the sum of `plastic` on one device may be relied on, other than what follows from the above.
Results may differ from a plain program's by a relative error of at most 0.0087.
Values may be sent and summed in bfloat16 or wider, within the bound.
No kernel may reach another device: no remote copies, remote signals or barrier semaphores. Data moves between devices by JAX's collectives and lax.ppermute only.
A program may use at most 64 MiB of HBM per device.

v0:
```python
import functools
import math

import jax
import jax.numpy as jnp
from jax import lax
from jax.experimental import pallas as pl
from jax.experimental.pallas import tpu as pltpu
from jax.sharding import PartitionSpec as P

STEP_SIZE = 0.5
SHEAR_MODULUS = 1.0
LAME_FIRST = 1.5
HARDENING = 0.5
YIELD_STRESS = 3.0
EPSILON = 1e-05
ITERS = 2
LANES = 128
SUB = 8
F32 = jnp.float32
BF16 = jnp.bfloat16


def grid_of(node_count, halo_count, elem_count):
    layers = node_count // halo_count
    assert layers == 2
    total = halo_count + 1 - elem_count // layers
    root = math.isqrt(total * total - 4 * halo_count)
    gx = (total + root) // 2
    gy = halo_count // gx
    assert gx * gy == halo_count and (gx - 1) * (gy - 1) * layers == elem_count
    assert gx == gy and gy % SUB == 0
    return gx, gy


def grid_index(p, gx, gy):
    nb = gy // SUB
    q, s = p // SUB, p % SUB
    return (nb * s + q // gx) * gx + q % gx


def column_of(row):
    n = row.shape[1]
    eye = lax.broadcasted_iota(jnp.int32, (n, n), 0) == lax.broadcasted_iota(jnp.int32, (n, n), 1)
    return jnp.sum(jnp.where(eye, row, 0.0), axis=1, keepdims=True)


def row_of(col):
    n = col.shape[0]
    eye = lax.broadcasted_iota(jnp.int32, (n, n), 0) == lax.broadcasted_iota(jnp.int32, (n, n), 1)
    return jnp.sum(jnp.where(eye, col, 0.0), axis=0, keepdims=True)


def split2(value):
    high = value.astype(BF16).astype(F32)
    return high, value - high


def first_layer_column(halo_row, gx, gy):
    n = gx * gy
    want = grid_index(lax.broadcasted_iota(jnp.int32, (n, n), 0), gx, gy)
    hit = lax.broadcasted_iota(jnp.int32, (n, n), 1) == want
    return jnp.sum(jnp.where(hit, halo_row, 0.0), axis=1, keepdims=True)


def select_rows(node_col, i, rows):
    n = node_col.shape[0]
    pick = (3.0 * node_col + i).astype(jnp.int32)
    return jnp.where(lax.broadcasted_iota(jnp.int32, (n, rows), 1) == pick, 1.0, 0.0).astype(BF16)


def scale_block(node_col, i, scale_row, tile, flag):
    n, tiles = node_col.shape[0], scale_row.shape[1]
    row = 3.0 * node_col + i
    low = lax.broadcasted_iota(jnp.int32, (n, tiles), 1).astype(F32) * tile
    scale = jnp.sum(jnp.where((row >= low) & (row < low + tile), scale_row, 0.0), axis=1, keepdims=True)
    high, rest = split2(scale)
    middle, last = split2(rest)
    lane = lax.broadcasted_iota(jnp.int32, (n, LANES), 1)
    return jnp.where(lane == 0, high, jnp.where(lane == 1, middle, jnp.where(lane == 2, last, jnp.where(lane == 3, flag, 0.0)))).astype(BF16)


def start_copies(sources, targets, sems):
    copies = [pltpu.make_async_copy(a, b, sems.at[i]) for i, (a, b) in enumerate(zip(sources, targets))]
    for copy in copies:
        copy.start()
    return copies


def spread_kernel(parts, coef_hbm, precond_hbm, out_ref, coef_ref, precond_ref, sems):
    owned, cases = coef_ref.shape
    per, spans = cases // parts, LANES // owned
    for copy in start_copies((coef_hbm, precond_hbm), (coef_ref, precond_ref), sems):
        copy.wait()
    high, low = split2(coef_ref[...])
    out_ref[:, :owned, :] = jnp.broadcast_to(high.astype(BF16)[None], (parts, owned, cases))
    mine = lax.rem(lax.axis_index("dom"), spans)
    lane = lax.broadcasted_iota(jnp.int32, (1, LANES), 1) // owned
    low = jnp.concatenate([low] * spans, axis=0).T
    low = jnp.where(lane == mine, low, 0.0).astype(BF16)
    rest = jnp.dot(unfold_matrix(parts, per, 0).T.astype(BF16), low, preferred_element_type=F32)
    scale = jnp.where(lane == mine, jnp.concatenate([precond_ref[...]] * spans, axis=1), 0.0)
    first, scale = split2(scale)
    second, third = split2(scale)
    row = lax.rem(lax.broadcasted_iota(jnp.int32, (parts * SUB, LANES), 0), SUB) - per
    rest = rest + jnp.where(row == 0, first, jnp.where(row == 1, second, jnp.where(row == 2, third, 0.0)))
    out_ref[:, owned:, :] = rest.reshape(parts, SUB, LANES).astype(BF16)


def unfold_matrix(parts, per, half):
    cases = parts * per
    c = lax.broadcasted_iota(jnp.int32, (cases, parts * SUB), 0)
    row = lax.broadcasted_iota(jnp.int32, (cases, parts * SUB), 1)
    return jnp.where(row == (c // per) * SUB + lax.rem(c, per) + half * per, 1.0, 0.0)


def setup_kernel(
    gx, gy, tile, halo_hbm, scale_hbm, conn_hbm, plastic_hbm, ext_hbm, basis_hbm,
    out_ref, ext_out, flag_row_ref, node_ref,
    ext_grid_ref, out_sems, halo_ref, scale_ref, conn_ref, plastic_ref, ext_ref, basis_ref, sems,
):
    n = gx * gy
    rows, rank = basis_ref.shape
    copies = start_copies(
        (halo_hbm, scale_hbm, conn_hbm, plastic_hbm, ext_hbm, basis_hbm),
        (halo_ref, scale_ref, conn_ref, plastic_ref, ext_ref, basis_ref),
        sems,
    )
    for copy in copies[:4]:
        copy.wait()
    conn = conn_ref[...].astype(F32)
    elems = conn.shape[1]
    place = grid_index(lax.broadcasted_iota(jnp.int32, (n, elems), 0), gx, gy).astype(F32) + 2 * n
    node0 = first_layer_column(halo_ref[...].astype(F32), gx, gy)
    node1 = jnp.full((n, 1), -1.0, F32)
    for corner in range(4):
        hit = conn[4 + corner : 5 + corner, :] == place
        found = jnp.max(jnp.where(hit, conn[corner : corner + 1, :], -1.0), axis=1, keepdims=True)
        node1 = jnp.maximum(node1, found)
    active = (plastic_ref[...] == 1).astype(F32)
    cells = (conn[0:1, :] == jnp.broadcast_to(node0, (n, elems)), conn[4:5, :] == place)
    flags = [jnp.max(jnp.where(hit, active, 0.0), axis=1, keepdims=True) for hit in cells]
    flag_row_ref[...] = jnp.zeros_like(flag_row_ref)
    flag = row_of(flags[1])
    for row in range(n // LANES):
        flag_row_ref[row : row + 1, :] = flag[:, row * LANES : (row + 1) * LANES]
    node_ref[...] = jnp.concatenate([row_of(node0), row_of(node1)], axis=1)
    copies[4].wait()
    high, low = split2(ext_ref[...])
    cases = ext_ref.shape[1]
    loads = jnp.concatenate([high.astype(BF16), low.astype(BF16)], axis=1)
    copies[5].wait()
    for layer, node in enumerate((node0, node1)):
        for i in range(3):
            start = (3 * layer + i) * n
            pick = select_rows(node, i, rows)
            both = jnp.dot(pick, loads, preferred_element_type=F32)
            ext_grid_ref[start : start + n, :] = both[:, :cases] + both[:, cases:]
            out_ref[start : start + n, rank:] = scale_block(node, i, scale_ref[...], tile, flags[layer])
            out_ref[start : start + n, :rank] = jnp.dot(
                pick, basis_ref[...], preferred_element_type=F32
            ).astype(BF16)
        if layer == 1:
            for copy in start_copies((ext_grid_ref,), (ext_out,), out_sems):
                copy.wait()


def cell_forces(gx, nb, flag_ref, below, above, add_below, add_above):
    quarter = 0.25
    n = gx * nb * SUB

    def load(ref, first, x, yb):
        start = first + (yb * gx + x) * SUB
        return ref[start : start + SUB, :]

    def level(x):
        total, jump = [], []
        for i in range(3):
            low = [load(below[0], below[1] + i * n, x, yb) for yb in range(nb)]
            high = [load(above[0], above[1] + i * n, x, yb) for yb in range(nb)]
            total.append([a + b for a, b in zip(low, high)])
            jump.append([b - a for a, b in zip(low, high)])
        return total, jump

    def roll_up(v):
        return pltpu.roll(v, SUB - 1, 0)

    def roll_down(v):
        return pltpu.roll(v, 1, 0)

    inside = lax.broadcasted_iota(jnp.int32, (SUB, LANES), 0) < SUB - 1
    total_modulus = 2.0 * SHEAR_MODULUS + HARDENING
    here = level(0)
    carry = None
    for x in range(gx - 1):
        there = level(x + 1)
        grad = [[[None] * 3 for _ in range(3)] for _ in range(nb)]
        for i in range(3):
            sum_x = [a + b for a, b in zip(here[0][i], there[0][i])]
            dif_x = [b - a for a, b in zip(here[0][i], there[0][i])]
            jmp_x = [a + b for a, b in zip(here[1][i], there[1][i])]
            sum_n = sum_x[1:] + [roll_up(sum_x[0])]
            dif_n = dif_x[1:] + [roll_up(dif_x[0])]
            jmp_n = jmp_x[1:] + [roll_up(jmp_x[0])]
            for yb in range(nb):
                grad[yb][i][0] = dif_x[yb] + dif_n[yb]
                grad[yb][i][1] = sum_n[yb] - sum_x[yb]
                grad[yb][i][2] = jmp_x[yb] + jmp_n[yb]
        stress = []
        for yb in range(nb):
            g = grad[yb]
            vol = (g[0][0] + g[1][1] + g[2][2]) * quarter
            third = vol * (2.0 * SHEAR_MODULUS / 3.0)
            diag = [g[i][i] * (2.0 * SHEAR_MODULUS * quarter) - third for i in range(3)]
            off = [
                (g[i][j] + g[j][i]) * (SHEAR_MODULUS * quarter) for i, j in ((0, 1), (0, 2), (1, 2))
            ]
            norm = diag[0] * diag[0] + diag[1] * diag[1] + diag[2] * diag[2]
            norm = norm + 2.0 * (off[0] * off[0] + off[1] * off[1] + off[2] * off[2])
            ratio = YIELD_STRESS * lax.rsqrt(jnp.maximum(norm, YIELD_STRESS * YIELD_STRESS))
            soft = HARDENING / total_modulus + (2.0 * SHEAR_MODULUS / total_modulus) * ratio
            factor = jnp.where(load(flag_ref, 0, x, yb) > 0.5, soft, 1.0)
            mean = LAME_FIRST * vol
            s = [None] * 6
            for i in range(3):
                s[i] = (mean + factor * diag[i]) * quarter
                s[3 + i] = factor * off[i] * quarter
            if yb == nb - 1:
                s = [jnp.where(inside, v, 0.0) for v in s]
            stress.append([[s[0], s[3], s[4]], [s[3], s[1], s[5]], [s[4], s[5], s[2]]])
        new_carry = []
        for i in range(3):
            ax = [stress[yb][i][0] for yb in range(nb)]
            ay = [stress[yb][i][1] for yb in range(nb)]
            az = [stress[yb][i][2] for yb in range(nb)]
            ax_p = [roll_down(ax[-1])] + ax[:-1]
            ay_p = [roll_down(ay[-1])] + ay[:-1]
            az_p = [roll_down(az[-1])] + az[:-1]
            for yb in range(nb):
                fx = ax_p[yb] + ax[yb]
                fy = ay_p[yb] - ay[yb]
                fz = az_p[yb] + az[yb]
                back, front = fy - fx, fy + fx
                low, high = back - fz, back + fz
                if carry is not None:
                    low, high = low + carry[i * nb + yb][0], high + carry[i * nb + yb][1]
                if add_below is not None:
                    add_below(i, x, yb, low)
                if add_above is not None:
                    add_above(i, x, yb, high)
                new_carry.append((front - fz, front + fz))
        carry = new_carry
        here = there
    for i in range(3):
        for yb in range(nb):
            if add_below is not None:
                add_below(i, gx - 1, yb, carry[i * nb + yb][0])
            if add_above is not None:
                add_above(i, gx - 1, yb, carry[i * nb + yb][1])


def along_lanes(block, first, count):
    lane = lax.broadcasted_iota(jnp.int32, (LANES, LANES), 0)
    mask = jnp.where((lane >= first) & (lane < first + count), 1.0, 0.0).astype(BF16)
    return jnp.dot(block, mask, preferred_element_type=F32)


def scale_of(block):
    return along_lanes(block, 0, 3)


def flag_of(basis_ref, layer, n):
    start = 3 * n * layer
    return along_lanes(basis_ref[start : start + n, basis_ref.shape[1] - LANES :], 3, 1)


def times_transposed(a, b):
    return lax.dot_general(a, b, (((1,), (1,)), ((), ())), preferred_element_type=F32)


def rows_of(layer, rows):
    return pl.ds(pl.multiple_of(layer * rows, rows), rows)


def lift_layer(folded, coef, basis_ref, layer, disp_ref, send_ref, flag_row_ref):
    rows, rank = basis_ref.shape[0] // 2, basis_ref.shape[1] - LANES
    block = basis_ref[rows_of(layer, rows), :]
    if folded:
        lifted = times_transposed(block[:, :rank], coef)
    else:
        lifted = jnp.dot(block[:, :rank], coef, preferred_element_type=F32)
    disp = lifted * scale_of(block[:, rank:])
    disp_ref[...] = disp
    send_ref[:rows, :] = disp.astype(BF16)
    send_ref[rows:, :] = flag_row_ref[...].astype(BF16)


def far_kernel(folded, source_ref, basis_ref, flag_row_ref, disp_ref, send_ref, coef_ref):
    rank = basis_ref.shape[1] - LANES
    if folded:
        parts, _, half = source_ref.shape
        coef = source_ref[...].reshape(parts * SUB, half)
        per = SUB * half // rank
        for part in range(2):
            turn = unfold_matrix(parts, per, part).astype(BF16)
            coef_ref[:, part * half : (part + 1) * half] = jnp.dot(
                turn, coef, preferred_element_type=F32
            ).astype(BF16)
    else:
        coef = source_ref[...] if source_ref.ndim == 2 else source_ref[:, : source_ref.shape[1] - SUB, :]
        coef_ref[...] = coef.reshape(coef_ref.shape)
    odd = lax.rem(lax.axis_index("dom"), 2)
    lift_layer(folded, coef_ref[...], basis_ref, odd, disp_ref, send_ref, flag_row_ref)


def near_kernel(folded, coef_ref, basis_ref, flag_row_ref, disp_ref, send_ref):
    odd = lax.rem(lax.axis_index("dom"), 2)
    lift_layer(folded, coef_ref[...], basis_ref, 1 - odd, disp_ref, send_ref, flag_row_ref)


def putter(gx, n, f_ref, layer):
    def put(i, x, yb, value):
        start = (3 * layer + i) * n + (yb * gx + x) * SUB
        f_ref[start : start + SUB, :] = value

    return put


def own_kernel(gx, gy, rank, prepare, far_ref, near_ref, basis_ref, *refs):
    if prepare:
        start_ref, disp_ref, force_ref, coef_ref, scale_ref, flag_ref = refs
    else:
        disp_ref, force_ref, flag_ref = refs
    n, nb = gx * gy, gy // SUB
    flag_ref[...] = flag_of(basis_ref, 0, n)
    even = lax.rem(lax.axis_index("dom"), 2) == 0
    far, near = far_ref[...], near_ref[...]
    disp_ref[: 3 * n, :] = jnp.where(even, far, near)
    disp_ref[3 * n :, :] = jnp.where(even, near, far)
    put = functools.partial(putter, gx, n, force_ref)
    cell_forces(gx, nb, flag_ref, (disp_ref, 0), (disp_ref, 3 * n), put(0), put(1))
    if prepare:
        parts, depth, cases = start_ref.shape
        owned, per, spans = depth - SUB, cases // parts, LANES * parts // rank
        me = lax.axis_index("dom")
        rest = start_ref[:, owned:, :].astype(F32)
        rest = [jnp.sum(rest[k * spans : (k + 1) * spans], axis=0) for k in range(parts // spans)]
        rest = jnp.concatenate(rest, axis=1)
        pick = lax.broadcasted_iota(jnp.int32, (SUB, cases), 0)
        lane = lax.broadcasted_iota(jnp.int32, (SUB, cases), 1)
        pick = jnp.where((lane == pick + me * per) & (pick < per), 1.0, 0.0).astype(BF16)
        high = times_transposed(pick, start_ref[:, :owned, :].reshape(rank, cases))
        scale = jnp.sum(rest[per : per + 3, :], axis=0, keepdims=True)
        scale_ref[...] = fold(jnp.broadcast_to(scale, (SUB, rank)))
        coef_ref[...] = fold(high + rest)


def side_cells(gx, gy, remote_ref, is_next, disp_ref, flag, side_ref, side_flag_ref, force_ref):
    n, nb = gx * gy, gy // SUB
    layer = 3 * n
    remote = remote_ref[...].astype(F32)
    side_ref[:layer, :] = jnp.where(is_next, disp_ref[layer:, :], remote[:layer, :])
    side_ref[layer:, :] = jnp.where(is_next, remote[:layer, :], disp_ref[:layer, :])
    for row in range(n // LANES):
        theirs = column_of(remote[layer + row : layer + row + 1, :])
        where = slice(row * LANES, (row + 1) * LANES)
        side_flag_ref[where, :] = jnp.where(is_next, flag[where, :], jnp.broadcast_to(theirs, (LANES, LANES)))
    chosen = jnp.broadcast_to(is_next, (SUB, LANES))
    put = putter(gx, n, force_ref, 0)
    lows = {}

    def keep(i, x, yb, value):
        lows[i, x, yb] = value

    def choose(i, x, yb, value):
        put(i, x, yb, jnp.where(chosen, lows.pop((i, x, yb)), value))

    cell_forces(gx, nb, side_flag_ref, (side_ref, 0), (side_ref, layer), keep, choose)


def project(resid, basis_ref, layer, parts, scaled_ref):
    rows = resid.shape[0]
    rank = basis_ref.shape[1] - LANES
    block = basis_ref[rows_of(layer, rows), :]
    scaled_ref[...] = (resid * scale_of(block[:, rank:])).astype(BF16)
    if parts is None:
        return jnp.dot(scaled_ref[...].astype(F32).T.astype(BF16), block[:, :rank], preferred_element_type=F32)
    half, per = rank // 2, resid.shape[1] // parts
    total = None
    for part in range(2):
        turn = unfold_matrix(parts, per, part).T.astype(BF16)
        turned = times_transposed(turn, scaled_ref[...]).astype(BF16)
        term = jnp.dot(turned, block[:, part * half : (part + 1) * half], preferred_element_type=F32)
        total = term if total is None else total + term
    return total


def side_kernel(
    gx, gy, parts, remote_ref, disp_ref, force_ref, basis_ref, ext_hbm,
    resid_ref, rest_ref, total_ref, side_ref, side_flag_ref, near_force_ref, scaled_ref, ext_ref, sems,
):
    layer = 3 * gx * gy
    copies = start_copies((ext_hbm,), (ext_ref,), sems)
    odd = lax.rem(lax.axis_index("dom"), 2)
    flag = flag_of(basis_ref, 1, gx * gy)
    side_cells(gx, gy, remote_ref, odd == 0, disp_ref, flag, side_ref, side_flag_ref, near_force_ref)
    copies[0].wait()
    near_rows, far_rows = rows_of(1 - odd, layer), rows_of(odd, layer)
    rest_ref[...] = ext_ref[far_rows, :] - force_ref[far_rows, :]
    resid_ref[...] = ext_ref[near_rows, :] - force_ref[near_rows, :] - near_force_ref[...]
    total_ref[...] = project(resid_ref[...], basis_ref, 1 - odd, parts, scaled_ref)


def sweep_kernel(gx, gy, parts, remote_ref, disp_ref, rest_ref, total_ref, basis_ref, *refs):
    part_ref, *resid_refs, side_ref, side_flag_ref, far_force_ref, scaled_ref = refs
    me = lax.axis_index("dom")
    odd = lax.rem(me, 2)
    flag = flag_of(basis_ref, 1, gx * gy)
    side_cells(gx, gy, remote_ref, odd == 1, disp_ref, flag, side_ref, side_flag_ref, far_force_ref)
    resid = rest_ref[...] - jnp.where(me > 0, far_force_ref[...], 0.0)
    for ref in resid_refs:
        ref[...] = resid
    total = total_ref[...] + project(resid, basis_ref, odd, parts, scaled_ref)
    part_ref[...] = total.reshape(part_ref.shape).astype(part_ref.dtype)


def fold(value):
    half = value.shape[1] // 2
    row = lax.broadcasted_iota(jnp.int32, (SUB, half), 0)
    return jnp.where(row < SUB // 2, value[:, :half], pltpu.roll(value[:, half:], SUB // 2, 0))


def step(coef, update, rank):
    square = jnp.broadcast_to(jnp.sum(update * update, axis=1, keepdims=True), (SUB, LANES))
    square = (square + pltpu.roll(square, SUB // 2, 0))[:, 0:1]
    return coef + STEP_SIZE * update * lax.rsqrt(square / rank + EPSILON)


def middle_kernel(rank, parts_ref, start_ref, scale_ref, coef_ref, send_ref):
    update = scale_ref[...] * jnp.sum(parts_ref[...].astype(F32), axis=0)
    coef = step(start_ref[...], update, rank)
    coef_ref[...] = coef
    send_ref[...] = jnp.broadcast_to(coef.astype(BF16)[None], send_ref.shape)


def last_kernel(rank, owned, parts_ref, coef_ref, scale_ref, send_ref):
    update = scale_ref[...] * jnp.sum(parts_ref[...].astype(F32), axis=0)
    coef = step(coef_ref[...], update, rank)
    parts, spans = send_ref.shape[0], LANES // owned
    half = SUB // 2
    place = lax.broadcasted_iota(jnp.int32, (SUB, LANES), 1) // owned
    column = lax.rem(lax.broadcasted_iota(jnp.int32, (SUB, LANES), 0), half)
    for block in range(coef.shape[1] // LANES):
        value = coef[:, block * LANES : (block + 1) * LANES]
        turned = [value] + [pltpu.roll(value, shift * owned, 1) for shift in range(1, spans)]
        for span in range(spans):
            line = jnp.zeros_like(value)
            for shift in range(spans):
                line = jnp.where(lax.rem(column + spans - span, spans) == shift, turned[shift], line)
            line = jnp.where(place == column, line, 0.0)
            device = block * spans + span
            send_ref[device] = jnp.sum(line[:half], axis=0, keepdims=True)
            send_ref[parts // 2 + device] = jnp.sum(line[half:], axis=0, keepdims=True)


def finish_kernel(got_ref, out_ref):
    owned, cases = out_ref.shape
    parts = got_ref.shape[0]
    per = cases // parts
    got = jnp.concatenate([got_ref[source] for source in range(parts)], axis=0)
    got = jnp.concatenate([got] * (LANES // parts), axis=0).T
    source = lax.broadcasted_iota(jnp.int32, (LANES, cases), 0)
    case = lax.broadcasted_iota(jnp.int32, (LANES, cases), 1)
    total = None
    for column in range(per):
        high, rest = split2(got[column * owned : (column + 1) * owned, :])
        middle, low = split2(rest)
        turn = jnp.where((source < parts) & (case == source * per + column), 1.0, 0.0).astype(BF16)
        for value in (high, middle, low):
            term = jnp.dot(value.astype(BF16), turn, preferred_element_type=F32)
            total = term if total is None else total + term
    out_ref[...] = total


def unpermute_kernel(gx, gy, node_ref, near_ref, far_ref, out_ref, parts_ref):
    n = gx * gy
    rows, cases = out_ref.shape
    odd = lax.rem(lax.axis_index("dom"), 2)
    for ref, layer in ((near_ref, 1 - odd), (far_ref, odd)):
        high, low = split2(ref[...])
        parts_ref[rows_of(layer, 3 * n), :cases] = high.astype(BF16)
        parts_ref[rows_of(layer, 3 * n), cases:] = low.astype(BF16)
    node = node_ref[...]
    target = jnp.concatenate(
        [3.0 * node[:, layer * n : (layer + 1) * n] + i for layer in range(2) for i in range(3)], axis=1
    ).astype(jnp.int32)
    step = rows // 3
    for start in range(0, rows, step):
        here = lax.broadcasted_iota(jnp.int32, (step, rows), 0) + start
        pick = jnp.where(here == target, 1.0, 0.0).astype(BF16)
        both = jnp.dot(pick, parts_ref[...], preferred_element_type=F32)
        out_ref[start : start + step, :] = both[:, :cases] + both[:, cases:]


def call(kernel, outs, scratch=(), hbm=(), hbm_out=(), vmem=24, flops=0, nbytes=0):
    def run(*operands):
        shapes = [operands[i].shape for i in hbm]
        operands = [
            pltpu.with_memory_space_constraint(value, pltpu.HBM) if i in hbm else value
            for i, value in enumerate(operands)
        ]
        spaces = [pltpu.HBM if i in hbm else pltpu.VMEM for i in range(len(operands))]
        places = [
            pl.BlockSpec(memory_space=pltpu.HBM if i in hbm_out else pltpu.VMEM)
            for i in range(len(outs) if isinstance(outs, tuple) else 1)
        ]
        return pl.pallas_call(
            kernel,
            out_shape=outs,
            in_specs=[pl.BlockSpec(memory_space=space) for space in spaces],
            out_specs=tuple(places) if isinstance(outs, tuple) else places[0],
            scratch_shapes=[
                *scratch,
                *[pltpu.VMEM(shape, operands[i].dtype) for i, shape in zip(hbm, shapes)],
                *([pltpu.SemaphoreType.DMA((len(hbm),))] if hbm else []),
            ],
            compiler_params=pltpu.CompilerParams(vmem_limit_bytes=vmem << 20),
            cost_estimate=pl.CostEstimate(flops=flops, bytes_accessed=nbytes, transcendentals=0),
        )(*operands)

    return run


def on_device(coef_init, basis, basis_scale, ext_force, precond, connectivity, halo_nodes, plastic):
    parts = lax.axis_size("dom")
    rows, cases = ext_force.shape
    rank = basis.shape[1]
    owned = coef_init.shape[0]
    n = halo_nodes.shape[0]
    elems = connectivity.shape[0]
    gx, gy = grid_of(rows // 3, n, elems)
    tile = rows // basis_scale.shape[0]
    half = rank // 2
    layer = 3 * n
    folded = parts * (SUB // 2) == cases and LANES % owned == 0 and owned * (SUB // 2) == LANES
    shape = jax.ShapeDtypeStruct
    scratch = pltpu.VMEM

    def exchange(value):
        return lax.all_to_all(value, "dom", 0, 0)

    if folded:
        start = exchange(
            call(
                functools.partial(spread_kernel, parts), shape((parts, owned + SUB, cases), BF16), hbm=(0, 1)
            )(coef_init, precond.reshape(1, owned))
        )
    else:
        coef = lax.all_gather(coef_init, "dom", axis=0, tiled=True)
        scaling = lax.all_gather(precond, "dom", axis=0, tiled=True)
    basis_grid, ext_grid, flag_row, nodes = call(
        functools.partial(setup_kernel, gx, gy, tile),
        (
            shape((rows, rank + LANES), BF16),
            pltpu.HBM((rows, cases), F32),
            shape((SUB, LANES), F32),
            shape((1, 2 * n), F32),
        ),
        [scratch((rows, cases), F32), pltpu.SemaphoreType.DMA((1,))],
        hbm=(0, 1, 2, 3, 4, 5),
        hbm_out=(1,),
        flops=2 * rows * rows * (rank + 2 * cases),
        nbytes=4 * rows * rank,
    )(
        halo_nodes.reshape(1, n),
        basis_scale.reshape(1, -1),
        connectivity.T,
        plastic.reshape(1, elems),
        ext_force,
        basis,
    )
    near_pairs = [(d, d ^ 1) for d in range(parts)]
    far_pairs = [pair for d in range(1, parts - 1, 2) for pair in ((d, d + 1), (d + 1, d))]
    layer_disp, layer_sent = shape((layer, cases), F32), shape((layer + SUB, cases), BF16)
    side_scratch = [scratch((2 * layer, cases), F32), scratch((n, LANES), F32)]
    columns = shape((SUB, half), F32)
    for sweep in range(ITERS):
        second, last = folded and sweep > 0, sweep == ITERS - 1
        source = (send if second else start) if folded else coef.astype(BF16)
        far_disp, far, coef_rows = call(
            functools.partial(far_kernel, second),
            (layer_disp, layer_sent, shape((cases, rank) if second else (rank, cases), BF16)),
            flops=rows * rank * cases,
        )(source, basis_grid, flag_row)
        far = lax.ppermute(far, "dom", far_pairs)
        near_disp, near = call(
            functools.partial(near_kernel, second), (layer_disp, layer_sent), flops=rows * rank * cases
        )(coef_rows, basis_grid, flag_row)
        near = lax.ppermute(near, "dom", near_pairs)
        prepare = folded and sweep == 0
        disp, force, *mine = call(
            functools.partial(own_kernel, gx, gy, rank, prepare),
            (shape((rows, cases), F32), shape((rows, cases), F32), *([columns] * 2 if prepare else [])),
            [scratch((n, LANES), F32)],
            flops=rows * rank * cases,
        )(far_disp, near_disp, basis_grid, *([start] if prepare else []))
        if prepare:
            coef_mine, scale_mine = mine
        cut = parts if folded else None
        total_shape = (parts * SUB, half) if folded else (cases, rank)
        layer_scratch = [*side_scratch, scratch((layer, cases), F32), scratch((layer, cases), BF16)]
        resid_near, rest, total = call(
            functools.partial(side_kernel, gx, gy, cut),
            (layer_disp, layer_disp, shape(total_shape, F32)),
            layer_scratch,
            hbm=(4,),
            flops=rows * rank * cases,
        )(near, disp, force, basis_grid, ext_grid)
        part_shape = shape((parts, SUB, half), BF16) if folded else shape((cases, rank), F32)
        part, *resid_far = call(
            functools.partial(sweep_kernel, gx, gy, cut),
            (part_shape, *([layer_disp] if last else [])),
            layer_scratch,
            flops=2 * rows * rank * cases,
        )(far, disp, rest, total, basis_grid)
        if folded:
            part = exchange(part)
            if not last:
                coef_mine, send = call(
                    functools.partial(middle_kernel, rank), (columns, shape(part.shape, BF16))
                )(part, coef_mine, scale_mine)
                send = exchange(send)
        else:
            update = scaling[:, None] * lax.psum(part, "dom").T
            root = jnp.sqrt(jnp.sum(update * update, axis=0) / rank + EPSILON)
            coef = coef + STEP_SIZE * update / root
    nodal_residual = call(
        functools.partial(unpermute_kernel, gx, gy),
        shape((rows, cases), F32),
        [scratch((rows, 2 * cases), BF16)],
        flops=2 * rows * rows * 2 * cases,
    )(nodes, resid_near, resid_far[0])
    if folded:
        sent = call(functools.partial(last_kernel, rank, owned), shape((parts, 1, LANES), F32))(
            part, coef_mine, scale_mine
        )
        coef_out = call(finish_kernel, shape((owned, cases), F32))(exchange(sent))
    else:
        coef_out = lax.dynamic_slice_in_dim(coef, lax.axis_index("dom") * owned, owned, 0)
    return coef_out, nodal_residual


def solution(mesh):
    return jax.shard_map(
        on_device,
        mesh=mesh,
        in_specs=(
            P("dom", None),
            P("dom", None),
            P("dom"),
            P("dom", None),
            P("dom"),
            P("dom", None),
            P("dom"),
            P("dom"),
        ),
        out_specs=(P("dom", None), P("dom", None)),
        check_vma=False,
    )
```

profile of v0, /device:TPU:0, one launch (start us, length us, event | category | flops | bytes accessed | tf_op | source)
XLA Modules:
  0.0 96.7 jit_solution(1297673440010512049)
XLA Ops:
  0.6 1.7 %shard_map.95 = bf16[32,40,128]{2,1,0:T(8,128)(2,1)} custom-call(f32[32,128]{1,0:T(8,128)} %coef_hbm.1, f32[1,32]{1,0:T(1,128)} %bitcast.5), custom_call_target="tpu_custom_call" | custom-call | tf_op jit(solution)/shard_map/pallas_call | solution.py:517
  2.4 7.4 %all-to-all-start = ((bf16[32,40,128]{2,1,0:T(8,128)(2,1)}), bf16[32,40,128]{2,1,0:T(8,128)(2,1)}, u32[]{:S(2)}, u32[]{:S(2)}) async-start(bf16[32,40,128]{2,1,0:T(8,128)(2,1)} %shard_map.95), calls=%async_computation | async-start | bytes 655360 | tf_op jit(solution)/shard_map/all_to_all | solution.py:550
  9.8 8.6 %shard_map.96 = (bf16[1536,1152]{1,0:T(8,128)(2,1)S(1)}, f32[1536,128]{1,0:T(8,128)}, f32[8,128]{1,0:T(8,128)S(1)}, f32[1,512]{1,0:T(1,128)S(1)}) custom-call(s32[1,256]{1,0:T(1,128)} %bitcast.8, f32[1,12]{1,0:T(1,128)} %bitcast.9, s32[8,450]{1,0:T(8,128)} %bitcast.6, s32[1,450]{1,0:T(1,128)} %bitcast.7, f32[1536,128]{1,0:T(8,128)} %ext_hbm.1, ...), custom_call_target="tpu_custom_call" | custom-call | flops 6039797760 | bytes 6291456 | tf_op jit(solution)/shard_map/pallas_call | solution.py:517
  18.5 3.4 %all-to-all-done.source_ref.refs_0_ = bf16[32,40,128]{2,1,0:T(8,128)(2,1)} async-done(((bf16[32,40,128]{2,1,0:T(8,128)(2,1)}), bf16[32,40,128]{2,1,0:T(8,128)(2,1)}, u32[]{:S(2)}, u32[]{:S(2)}) %all-to-all-start) | async-done | bytes 327712 | tf_op jit(solution)/shard_map/all_to_all | solution.py:550
  21.9 1.6 %shard_map.97 = (f32[768,128]{1,0:T(8,128)S(1)}, bf16[776,128]{1,0:T(8,128)(2,1)S(1)}, bf16[1024,128]{1,0:T(8,128)(2,1)S(1)}) custom-call(bf16[32,40,128]{2,1,0:T(8,128)(2,1)} %all-to-all-done.source_ref.refs_0_, bf16[1536,1152]{1,0:T(8,128)(2,1)S(1)} %get-tuple-element.31.basis_ref, f32[8,128]{1,0:T(8,128)S(1)} %get-tuple-element.32.flag_row_ref), custom_call_target="tpu_custom_call" | custom-call | flops 201326592 | tf_op jit(solution)/shard_map/pallas_call | solution.py:517
  24.2 0.7 collective-permute-start
  24.9 1.6 %shard_map.99 = (f32[1536,128]{1,0:T(8,128)S(1)}, f32[1536,128]{1,0:T(8,128)S(1)}, f32[8,512]{1,0:T(8,128)S(1)}, f32[8,512]{1,0:T(8,128)S(1)}) custom-call(f32[768,128]{1,0:T(8,128)S(1)} %get-tuple-element.34.far_ref, f32[768,128]{1,0:T(8,128)S(1)} %get-tuple-element.36.near_ref, bf16[1536,1152]{1,0:T(8,128)(2,1)S(1)} %get-tuple-element.31.basis_ref, ...), custom_call_target="tpu_custom_call" | custom-call | flops 201326592 | tf_op jit(solution)/shard_map/pallas_call | solution.py:517
  26.5 2.4 %shard_map.100 = (f32[768,128]{1,0:T(8,128)}, f32[768,128]{1,0:T(8,128)S(1)}, f32[256,512]{1,0:T(8,128)S(1)}) custom-call(bf16[776,128]{1,0:T(8,128)(2,1)S(1)} %collective-permute-done.1.remote_ref, f32[1536,128]{1,0:T(8,128)S(1)} %get-tuple-element.37.disp_ref, f32[1536,128]{1,0:T(8,128)S(1)} %get-tuple-element.39.force_ref, ...), custom_call_target="tpu_custom_call" | custom-call | flops 201326592 | tf_op jit(solution)/shard_map/pallas_call | solution.py:517
  28.9 1.5 %shard_map.101 = bf16[32,8,512]{2,1,0:T(8,128)(2,1)S(1)} custom-call(bf16[776,128]{1,0:T(8,128)(2,1)S(1)} %collective-permute-done.remote_ref, f32[1536,128]{1,0:T(8,128)S(1)} %get-tuple-element.37.disp_ref, f32[768,128]{1,0:T(8,128)S(1)} %get-tuple-element.41.rest_ref, f32[256,512]{1,0:T(8,128)S(1)} %get-tuple-element.42.total_ref, ...), custom_call_target="tpu_custom_call" | custom-call | flops 402653184 | tf_op jit(solution)/shard_map/pallas_call | solution.py:517
  30.4 16.9 %all_to_all.25.parts_ref = bf16[32,8,512]{2,1,0:T(8,128)(2,1)S(1)} all-to-all(bf16[32,8,512]{2,1,0:T(8,128)(2,1)S(1)} %shard_map.101), channel_id=1, replica_groups=mesh['dom'=32] {'dom'}, dimensions={0} | all-to-all | bytes 524288 | tf_op jit(solution)/shard_map/all_to_all | solution.py:550
  47.6 12.8 %all_to_all.26.source_ref = bf16[32,8,512]{2,1,0:T(8,128)(2,1)S(1)} all-to-all(bf16[32,8,512]{2,1,0:T(8,128)(2,1)S(1)} %get-tuple-element.45), channel_id=1, replica_groups=mesh['dom'=32] {'dom'}, dimensions={0} | all-to-all | bytes 524288 | tf_op jit(solution)/shard_map/all_to_all | solution.py:550
  60.3 0.8 shard_map.103
  61.8 0.7 collective-permute-start.2
  63.3 2.4 %shard_map.106 = (f32[768,128]{1,0:T(8,128)S(1)}, f32[768,128]{1,0:T(8,128)S(1)}, f32[256,512]{1,0:T(8,128)S(1)}) custom-call(bf16[776,128]{1,0:T(8,128)(2,1)S(1)} %collective-permute-done.3.remote_ref, f32[1536,128]{1,0:T(8,128)S(1)} %get-tuple-element.50.disp_ref, f32[1536,128]{1,0:T(8,128)S(1)} %get-tuple-element.52.force_ref, ...), custom_call_target="tpu_custom_call" | custom-call | flops 201326592 | tf_op jit(solution)/shard_map/pallas_call | solution.py:517
  65.7 0.7 copy-done
  66.4 1.5 %shard_map.107 = (bf16[32,8,512]{2,1,0:T(8,128)(2,1)S(1)}, f32[768,128]{1,0:T(8,128)S(1)}) custom-call(bf16[776,128]{1,0:T(8,128)(2,1)S(1)} %collective-permute-done.2.remote_ref, f32[1536,128]{1,0:T(8,128)S(1)} %get-tuple-element.50.disp_ref, f32[768,128]{1,0:T(8,128)S(1)} %get-tuple-element.53.rest_ref, f32[256,512]{1,0:T(8,128)S(1)} %get-tuple-element.54.total_ref, ...), custom_call_target="tpu_custom_call" | custom-call | flops 402653184 | tf_op jit(solution)/shard_map/pallas_call | solution.py:517
  67.9 17.3 %all_to_all.27.parts_ref = bf16[32,8,512]{2,1,0:T(8,128)(2,1)S(1)} all-to-all(bf16[32,8,512]{2,1,0:T(8,128)(2,1)S(1)} %get-tuple-element.55), channel_id=1, replica_groups=mesh['dom'=32] {'dom'}, dimensions={0} | all-to-all | bytes 524288 | tf_op jit(solution)/shard_map/all_to_all | solution.py:550
  85.2 0.9 shard_map.108
  86.2 2.5 %all-to-all-start.4 = ((f32[32,1,128]{2,1,0:T(1,128)}), f32[32,1,128]{2,1,0:T(1,128)S(1)}, u32[]{:S(2)}, u32[]{:S(2)}) async-start(f32[32,1,128]{2,1,0:T(1,128)} %shard_map.108), calls=%async_computation.4 | async-start | bytes 32768 | tf_op jit(solution)/shard_map/all_to_all | solution.py:550
  88.7 1.0 %copy-done.1 = f32[768,128]{1,0:T(8,128)S(1)} copy-done((f32[768,128]{1,0:T(8,128)S(1)}, f32[768,128]{1,0:T(8,128)}, u32[]{:S(2)}) %copy-start.1) | copy-done | bytes 393240
  89.7 1.0 %copy-done.3 = f32[768,128]{1,0:T(8,128)S(1)} copy-done((f32[768,128]{1,0:T(8,128)S(1)}, f32[768,128]{1,0:T(8,128)}, u32[]{:S(2)}) %copy-start.3) | copy-done | bytes 393240
  90.7 2.5 %shard_map.110 = f32[1536,128]{1,0:T(8,128)} custom-call(f32[1,512]{1,0:T(1,128)S(1)} %get-tuple-element.57.node_ref, f32[768,128]{1,0:T(8,128)S(1)} %copy-done.1, f32[768,128]{1,0:T(8,128)S(1)} %copy-done.3), custom_call_target="tpu_custom_call" | custom-call | flops 1207959552 | tf_op jit(solution)/shard_map/pallas_call | solution.py:517
  93.2 2.6 %all-to-all-done.4.got_ref = f32[32,1,128]{2,1,0:T(1,128)S(1)} async-done(((f32[32,1,128]{2,1,0:T(1,128)}), f32[32,1,128]{2,1,0:T(1,128)S(1)}, u32[]{:S(2)}, u32[]{:S(2)}) %all-to-all-start.4) | async-done | bytes 16416 | tf_op jit(solution)/shard_map/all_to_all | solution.py:550
  95.8 0.9 shard_map.109
  (15 shorter events, 2.4 us)
Async XLA Ops:
  2.4 19.5 %all-to-all-start = ((bf16[32,40,128]{2,1,0:T(8,128)(2,1)}), bf16[32,40,128]{2,1,0:T(8,128)(2,1)}, u32[]{:S(2)}, u32[]{:S(2)}) async-start(bf16[32,40,128]{2,1,0:T(8,128)(2,1)} %shard_map.95), calls=%async_computation | async-start | bytes 655360 | tf_op jit(solution)/shard_map/all_to_all | solution.py:550
  24.1 2.4 %collective-permute-start.1 = (bf16[776,128]{1,0:T(8,128)(2,1)S(1)}, bf16[776,128]{1,0:T(8,128)(2,1)S(1)}, u32[]{:S(2)}, u32[]{:S(2)}) collective-permute-start(bf16[776,128]{1,0:T(8,128)(2,1)S(1)} %get-tuple-element.38), channel_id=1, source_target_pairs={{0,1},{1,0},{2,3},{3,2},{4,5},{5,4},{6,7},{7,6},{8,9},{9,8},{10,11... | collective-permute-start | bytes 595976 | tf_op jit(solution)/shard_map/ppermute | solution.py:599
  24.2 4.7 %collective-permute-start = (bf16[776,128]{1,0:T(8,128)(2,1)S(1)}, bf16[776,128]{1,0:T(8,128)(2,1)S(1)}, u32[]{:S(2)}, u32[]{:S(2)}) collective-permute-start(bf16[776,128]{1,0:T(8,128)(2,1)S(1)} %get-tuple-element.33), channel_id=1, source_target_pairs={{1,2},{2,1},{3,4},{4,3},{5,6},{6,5},{7,8},{8,7},{9,10},{10,9},{11,... | collective-permute-start | bytes 595976 | tf_op jit(solution)/shard_map/ppermute | solution.py:595
  61.8 1.5 %collective-permute-start.3 = (bf16[776,128]{1,0:T(8,128)(2,1)S(1)}, bf16[776,128]{1,0:T(8,128)(2,1)S(1)}, u32[]{:S(2)}, u32[]{:S(2)}) collective-permute-start(bf16[776,128]{1,0:T(8,128)(2,1)S(1)} %get-tuple-element.51), channel_id=1, source_target_pairs={{0,1},{1,0},{2,3},{3,2},{4,5},{5,4},{6,7},{7,6},{8,9},{9,8},{10,11... | collective-permute-start | bytes 595976 | tf_op jit(solution)/shard_map/ppermute | solution.py:599
  61.8 4.6 %collective-permute-start.2 = (bf16[776,128]{1,0:T(8,128)(2,1)S(1)}, bf16[776,128]{1,0:T(8,128)(2,1)S(1)}, u32[]{:S(2)}, u32[]{:S(2)}) collective-permute-start(bf16[776,128]{1,0:T(8,128)(2,1)S(1)} %get-tuple-element.46), channel_id=1, source_target_pairs={{1,2},{2,1},{3,4},{4,3},{5,6},{6,5},{7,8},{8,7},{9,10},{10,9},{11,... | collective-permute-start | bytes 595976 | tf_op jit(solution)/shard_map/ppermute | solution.py:595
  65.7 0.7 copy-start
  67.9 17.3 %copy-start.2 = (f32[768,128]{1,0:T(8,128)}, f32[768,128]{1,0:T(8,128)S(1)}, u32[]{:S(2)}) copy-start(f32[768,128]{1,0:T(8,128)S(1)} %get-tuple-element.59.far_ref) | copy-start | bytes 1179652
  86.2 9.7 %all-to-all-start.4 = ((f32[32,1,128]{2,1,0:T(1,128)}), f32[32,1,128]{2,1,0:T(1,128)S(1)}, u32[]{:S(2)}, u32[]{:S(2)}) async-start(f32[32,1,128]{2,1,0:T(1,128)} %shard_map.108), calls=%async_computation.4 | async-start | bytes 32768 | tf_op jit(solution)/shard_map/all_to_all | solution.py:550
  88.7 1.0 %copy-start.1 = (f32[768,128]{1,0:T(8,128)S(1)}, f32[768,128]{1,0:T(8,128)}, u32[]{:S(2)}) copy-start(f32[768,128]{1,0:T(8,128)} %copy-done) | copy-start | bytes 1179652
  89.7 1.0 %copy-start.3 = (f32[768,128]{1,0:T(8,128)S(1)}, f32[768,128]{1,0:T(8,128)}, u32[]{:S(2)}) copy-start(f32[768,128]{1,0:T(8,128)} %copy-done.2) | copy-start | bytes 1179652
where the time goes:
time: 97.3 us; the launch traced here: 96.7 us
  blocking collectives  47 us (48%)
  Pallas kernels  28.5 us (29%)
  starting transfers between devices  11.5 us (12%)
  waiting for transfers between devices  6.16 us (6%)
  local copies, waits for them, and re-layouts  2.73 us (3%)
    all_to_all x3, blocking collectives, exchange(): return lax.all_to_all(value, 'dom', 0, 0)  47 us
    pallas_call x16, Pallas kernels, run(): pl.pallas_call(kernel, out_shape=outs, in_specs=[pl.BlockSpec(memory_spac...  28.5 us
    all_to_all x2, starting transfers between devices, exchange(): return lax.all_to_all(value, 'dom', 0, 0)  9.99 us
    all_to_all x2, waiting for transfers between devices, exchange(): return lax.all_to_all(value, 'dom', 0, 0)  6.03 us
    unnamed x8, local copies, waits for them, and re-layouts  2.73 us
  transfers between devices with their start and end apart: 6, of which 3 were waited for; matrix products, arithmetic and copies ran while one was open for 0% of the time, Pallas kernels for 19%

commit v1 on v0

--- a/solution.py
+++ b/solution.py
@@ -69,15 +69,18 @@
     return jnp.where(lax.broadcasted_iota(jnp.int32, (n, rows), 1) == pick, 1.0, 0.0).astype(BF16)
 
 
-def scale_block(node_col, i, scale_row, tile, flag):
-    n, tiles = node_col.shape[0], scale_row.shape[1]
-    row = 3.0 * node_col + i
-    low = lax.broadcasted_iota(jnp.int32, (n, tiles), 1).astype(F32) * tile
-    scale = jnp.sum(jnp.where((row >= low) & (row < low + tile), scale_row, 0.0), axis=1, keepdims=True)
+def scale_block(node_row, i, scale_col, tile, flag_row):
+    tiles, n = scale_col.shape[0], node_row.shape[1]
+    row = 3.0 * node_row + i
+    low = lax.broadcasted_iota(jnp.int32, (tiles, n), 0).astype(F32) * tile
+    scale = jnp.sum(jnp.where((row >= low) & (row < low + tile), scale_col, 0.0), axis=0, keepdims=True)
     high, rest = split2(scale)
     middle, last = split2(rest)
-    lane = lax.broadcasted_iota(jnp.int32, (n, LANES), 1)
-    return jnp.where(lane == 0, high, jnp.where(lane == 1, middle, jnp.where(lane == 2, last, jnp.where(lane == 3, flag, 0.0)))).astype(BF16)
+    place = lax.broadcasted_iota(jnp.int32, (SUB, n), 0)
+    block = jnp.zeros((SUB, n), F32)
+    for index, value in enumerate((high, middle, last, flag_row)):
+        block = jnp.where(place == index, value, block)
+    return block.astype(BF16)
 
 
 def start_copies(sources, targets, sems):
@@ -87,24 +90,29 @@
     return copies
 
 
-def spread_kernel(parts, coef_hbm, precond_hbm, out_ref, coef_ref, precond_ref, sems):
+def spread_kernel(parts, coef_hbm, precond_hbm, out_hbm, high_ref, rest_ref, out_sems, coef_ref, precond_ref, sems):
     owned, cases = coef_ref.shape
     per, spans = cases // parts, LANES // owned
     for copy in start_copies((coef_hbm, precond_hbm), (coef_ref, precond_ref), sems):
         copy.wait()
     high, low = split2(coef_ref[...])
-    out_ref[:, :owned, :] = jnp.broadcast_to(high.astype(BF16)[None], (parts, owned, cases))
+    high_ref[...] = jnp.broadcast_to(high.astype(BF16)[None], (parts, owned, cases))
+    (high_copy,) = start_copies((high_ref,), (out_hbm.at[:, :owned, :],), out_sems)
     mine = lax.rem(lax.axis_index("dom"), spans)
     lane = lax.broadcasted_iota(jnp.int32, (1, LANES), 1) // owned
     low = jnp.concatenate([low] * spans, axis=0).T
     low = jnp.where(lane == mine, low, 0.0).astype(BF16)
-    rest = jnp.dot(unfold_matrix(parts, per, 0).T.astype(BF16), low, preferred_element_type=F32)
+    rest = jnp.dot(fold_matrix(parts, per, 0), low, preferred_element_type=F32)
     scale = jnp.where(lane == mine, jnp.concatenate([precond_ref[...]] * spans, axis=1), 0.0)
     first, scale = split2(scale)
     second, third = split2(scale)
     row = lax.rem(lax.broadcasted_iota(jnp.int32, (parts * SUB, LANES), 0), SUB) - per
     rest = rest + jnp.where(row == 0, first, jnp.where(row == 1, second, jnp.where(row == 2, third, 0.0)))
-    out_ref[:, owned:, :] = rest.reshape(parts, SUB, LANES).astype(BF16)
+    rest_ref[...] = rest.reshape(parts, SUB, LANES).astype(BF16)
+    rest_copy = pltpu.make_async_copy(rest_ref, out_hbm.at[:, owned:, :], out_sems.at[1])
+    rest_copy.start()
+    high_copy.wait()
+    rest_copy.wait()
 
 
 def unfold_matrix(parts, per, half):
@@ -114,13 +122,21 @@
     return jnp.where(row == (c // per) * SUB + lax.rem(c, per) + half * per, 1.0, 0.0)
 
 
+def fold_matrix(parts, per, half):
+    row = lax.broadcasted_iota(jnp.int32, (parts * SUB, parts * per), 0)
+    case = lax.broadcasted_iota(jnp.int32, (parts * SUB, parts * per), 1)
+    place = row % SUB - half * per
+    here = (place >= 0) & (place < per) & (case == row // SUB * per + place)
+    return jnp.where(here, 1.0, 0.0).astype(BF16)
+
+
 def setup_kernel(
     gx, gy, tile, halo_hbm, scale_hbm, conn_hbm, plastic_hbm, ext_hbm, basis_hbm,
-    out_ref, ext_out, flag_row_ref, node_ref,
+    out_ref, scale_out_ref, ext_out, flag_row_ref, node_ref,
     ext_grid_ref, out_sems, halo_ref, scale_ref, conn_ref, plastic_ref, ext_ref, basis_ref, sems,
 ):
     n = gx * gy
-    rows, rank = basis_ref.shape
+    rows, _ = basis_ref.shape
     copies = start_copies(
         (halo_hbm, scale_hbm, conn_hbm, plastic_hbm, ext_hbm, basis_hbm),
         (halo_ref, scale_ref, conn_ref, plastic_ref, ext_ref, basis_ref),
@@ -141,28 +157,39 @@
     cells = (conn[0:1, :] == jnp.broadcast_to(node0, (n, elems)), conn[4:5, :] == place)
     flags = [jnp.max(jnp.where(hit, active, 0.0), axis=1, keepdims=True) for hit in cells]
     flag_row_ref[...] = jnp.zeros_like(flag_row_ref)
-    flag = row_of(flags[1])
+    flag_rows = [row_of(flag) for flag in flags]
+    flag = flag_rows[1]
+    scale_col = column_of(scale_ref[...])
+    node_rows = [row_of(node0), row_of(node1)]
     for row in range(n // LANES):
         flag_row_ref[row : row + 1, :] = flag[:, row * LANES : (row + 1) * LANES]
-    node_ref[...] = jnp.concatenate([row_of(node0), row_of(node1)], axis=1)
+    node_ref[...] = jnp.concatenate(node_rows, axis=1)
     copies[4].wait()
     high, low = split2(ext_ref[...])
     cases = ext_ref.shape[1]
     loads = jnp.concatenate([high.astype(BF16), low.astype(BF16)], axis=1)
     copies[5].wait()
+    out_copies = []
     for layer, node in enumerate((node0, node1)):
         for i in range(3):
             start = (3 * layer + i) * n
             pick = select_rows(node, i, rows)
             both = jnp.dot(pick, loads, preferred_element_type=F32)
             ext_grid_ref[start : start + n, :] = both[:, :cases] + both[:, cases:]
-            out_ref[start : start + n, rank:] = scale_block(node, i, scale_ref[...], tile, flags[layer])
-            out_ref[start : start + n, :rank] = jnp.dot(
+            if i == 2:
+                done = slice(3 * n * layer, 3 * n * (layer + 1))
+                out_copies.append(
+                    pltpu.make_async_copy(ext_grid_ref.at[done, :], ext_out.at[done, :], out_sems.at[layer])
+                )
+                out_copies[-1].start()
+            scale_out_ref[layer, :, i * n : (i + 1) * n] = scale_block(
+                node_rows[layer], i, scale_col, tile, flag_rows[layer]
+            )
+            out_ref[start : start + n, :] = jnp.dot(
                 pick, basis_ref[...], preferred_element_type=F32
             ).astype(BF16)
-        if layer == 1:
-            for copy in start_copies((ext_grid_ref,), (ext_out,), out_sems):
-                copy.wait()
+    for copy in out_copies:
+        copy.wait()
 
 
 def cell_forces(gx, nb, flag_ref, below, above, add_below, add_above):
@@ -260,18 +287,17 @@
 
 
 def along_lanes(block, first, count):
-    lane = lax.broadcasted_iota(jnp.int32, (LANES, LANES), 0)
-    mask = jnp.where((lane >= first) & (lane < first + count), 1.0, 0.0).astype(BF16)
-    return jnp.dot(block, mask, preferred_element_type=F32)
-
-
-def scale_of(block):
-    return along_lanes(block, 0, 3)
-
-
-def flag_of(basis_ref, layer, n):
-    start = 3 * n * layer
-    return along_lanes(basis_ref[start : start + n, basis_ref.shape[1] - LANES :], 3, 1)
+    row = lax.broadcasted_iota(jnp.int32, (SUB, LANES), 0)
+    mask = jnp.where((row >= first) & (row < first + count), 1.0, 0.0).astype(BF16)
+    return lax.dot_general(block, mask, (((0,), (0,)), ((), ())), preferred_element_type=F32)
+
+
+def scale_of(scale_ref, layer):
+    return along_lanes(scale_ref[layer], 0, 3)
+
+
+def flag_of(scale_ref, layer, n):
+    return along_lanes(scale_ref[layer, :, :n], 3, 1)
 
 
 def times_transposed(a, b):
@@ -282,40 +308,44 @@
     return pl.ds(pl.multiple_of(layer * rows, rows), rows)
 
 
-def lift_layer(folded, coef, basis_ref, layer, disp_ref, send_ref, flag_row_ref):
-    rows, rank = basis_ref.shape[0] // 2, basis_ref.shape[1] - LANES
+def lift_layer(folded, coef, basis_ref, scale_ref, layer, disp_ref, send_ref, flag_row_ref):
+    rows = basis_ref.shape[0] // 2
     block = basis_ref[rows_of(layer, rows), :]
     if folded:
-        lifted = times_transposed(block[:, :rank], coef)
+        lifted = times_transposed(block, coef)
     else:
-        lifted = jnp.dot(block[:, :rank], coef, preferred_element_type=F32)
-    disp = lifted * scale_of(block[:, rank:])
+        lifted = jnp.dot(block, coef, preferred_element_type=F32)
+    disp = lifted * scale_of(scale_ref, layer)
     disp_ref[...] = disp
     send_ref[:rows, :] = disp.astype(BF16)
     send_ref[rows:, :] = flag_row_ref[...].astype(BF16)
 
 
-def far_kernel(folded, source_ref, basis_ref, flag_row_ref, disp_ref, send_ref, coef_ref):
-    rank = basis_ref.shape[1] - LANES
-    if folded:
-        parts, _, half = source_ref.shape
-        coef = source_ref[...].reshape(parts * SUB, half)
-        per = SUB * half // rank
-        for part in range(2):
-            turn = unfold_matrix(parts, per, part).astype(BF16)
-            coef_ref[:, part * half : (part + 1) * half] = jnp.dot(
-                turn, coef, preferred_element_type=F32
-            ).astype(BF16)
-    else:
-        coef = source_ref[...] if source_ref.ndim == 2 else source_ref[:, : source_ref.shape[1] - SUB, :]
-        coef_ref[...] = coef.reshape(coef_ref.shape)
+def far_kernel(same_ref, other_ref, basis_ref, scale_ref, flag_row_ref, disp_ref, send_ref, coef_ref, source_ref):
+    rank = basis_ref.shape[1]
+    chips, _, half = same_ref.shape
+    core = lax.rem(lax.axis_index("dom"), 2)
+    source_ref[:, core] = same_ref[...]
+    source_ref[:, 1 - core] = other_ref[...]
+    coef = source_ref[...].reshape(chips * 2 * SUB, half)
+    per = SUB * half // rank
+    for part in range(2):
+        turn = unfold_matrix(2 * chips, per, part).astype(BF16)
+        coef_ref[:, part * half : (part + 1) * half] = jnp.dot(
+            turn, coef, preferred_element_type=F32
+        ).astype(BF16)
+    lift_layer(True, coef_ref[...], basis_ref, scale_ref, core, disp_ref, send_ref, flag_row_ref)
+
+
+def first_far_kernel(owned, source_ref, basis_ref, scale_ref, flag_row_ref, disp_ref, send_ref, coef_ref):
+    coef_ref[...] = source_ref[:, :owned, :].reshape(coef_ref.shape)
     odd = lax.rem(lax.axis_index("dom"), 2)
-    lift_layer(folded, coef_ref[...], basis_ref, odd, disp_ref, send_ref, flag_row_ref)
-
-
-def near_kernel(folded, coef_ref, basis_ref, flag_row_ref, disp_ref, send_ref):
+    lift_layer(False, coef_ref[...], basis_ref, scale_ref, odd, disp_ref, send_ref, flag_row_ref)
+
+
+def near_kernel(folded, coef_ref, basis_ref, scale_ref, flag_row_ref, disp_ref, send_ref):
     odd = lax.rem(lax.axis_index("dom"), 2)
-    lift_layer(folded, coef_ref[...], basis_ref, 1 - odd, disp_ref, send_ref, flag_row_ref)
+    lift_layer(folded, coef_ref[...], basis_ref, scale_ref, 1 - odd, disp_ref, send_ref, flag_row_ref)
 
 
 def putter(gx, n, f_ref, layer):
@@ -326,13 +356,13 @@
     return put
 
 
-def own_kernel(gx, gy, rank, prepare, far_ref, near_ref, basis_ref, *refs):
+def own_kernel(gx, gy, rank, prepare, far_ref, near_ref, scale_in_ref, *refs):
     if prepare:
         start_ref, disp_ref, force_ref, coef_ref, scale_ref, flag_ref = refs
     else:
         disp_ref, force_ref, flag_ref = refs
     n, nb = gx * gy, gy // SUB
-    flag_ref[...] = flag_of(basis_ref, 0, n)
+    flag_ref[...] = flag_of(scale_in_ref, 0, n)
     even = lax.rem(lax.axis_index("dom"), 2) == 0
     far, near = far_ref[...], near_ref[...]
     disp_ref[: 3 * n, :] = jnp.where(even, far, near)
@@ -378,17 +408,17 @@
     cell_forces(gx, nb, side_flag_ref, (side_ref, 0), (side_ref, layer), keep, choose)
 
 
-def project(resid, basis_ref, layer, parts, scaled_ref):
+def project(resid, basis_ref, scale_ref, layer, parts, scaled_ref):
     rows = resid.shape[0]
-    rank = basis_ref.shape[1] - LANES
+    rank = basis_ref.shape[1]
     block = basis_ref[rows_of(layer, rows), :]
-    scaled_ref[...] = (resid * scale_of(block[:, rank:])).astype(BF16)
+    scaled_ref[...] = (resid * scale_of(scale_ref, layer)).astype(BF16)
     if parts is None:
-        return jnp.dot(scaled_ref[...].astype(F32).T.astype(BF16), block[:, :rank], preferred_element_type=F32)
+        return jnp.dot(scaled_ref[...].astype(F32).T.astype(BF16), block, preferred_element_type=F32)
     half, per = rank // 2, resid.shape[1] // parts
     total = None
     for part in range(2):
-        turn = unfold_matrix(parts, per, part).T.astype(BF16)
+        turn = fold_matrix(parts, per, part)
         turned = times_transposed(turn, scaled_ref[...]).astype(BF16)
         term = jnp.dot(turned, block[:, part * half : (part + 1) * half], preferred_element_type=F32)
         total = term if total is None else total + term
@@ -396,32 +426,36 @@
 
 
 def side_kernel(
-    gx, gy, parts, remote_ref, disp_ref, force_ref, basis_ref, ext_hbm,
-    resid_ref, rest_ref, total_ref, side_ref, side_flag_ref, near_force_ref, scaled_ref, ext_ref, sems,
+    gx, gy, parts, remote_ref, disp_ref, force_ref, basis_ref, scale_ref, ext_hbm,
+    resid_hbm, rest_ref, total_ref, side_ref, side_flag_ref, near_force_ref, scaled_ref, resid_ref, out_sems, ext_ref, sems,
 ):
     layer = 3 * gx * gy
     copies = start_copies((ext_hbm,), (ext_ref,), sems)
     odd = lax.rem(lax.axis_index("dom"), 2)
-    flag = flag_of(basis_ref, 1, gx * gy)
+    flag = flag_of(scale_ref, 1, gx * gy)
     side_cells(gx, gy, remote_ref, odd == 0, disp_ref, flag, side_ref, side_flag_ref, near_force_ref)
     copies[0].wait()
     near_rows, far_rows = rows_of(1 - odd, layer), rows_of(odd, layer)
     rest_ref[...] = ext_ref[far_rows, :] - force_ref[far_rows, :]
     resid_ref[...] = ext_ref[near_rows, :] - force_ref[near_rows, :] - near_force_ref[...]
-    total_ref[...] = project(resid_ref[...], basis_ref, 1 - odd, parts, scaled_ref)
-
-
-def sweep_kernel(gx, gy, parts, remote_ref, disp_ref, rest_ref, total_ref, basis_ref, *refs):
-    part_ref, *resid_refs, side_ref, side_flag_ref, far_force_ref, scaled_ref = refs
+    out_copies = start_copies((resid_ref,), (resid_hbm,), out_sems)
+    total_ref[...] = project(resid_ref[...], basis_ref, scale_ref, 1 - odd, parts, scaled_ref)
+    out_copies[0].wait()
+
+
+def sweep_kernel(gx, gy, parts, remote_ref, disp_ref, rest_ref, total_ref, basis_ref, scale_ref, *refs):
+    part_ref, *resid_hbm, side_ref, side_flag_ref, far_force_ref, scaled_ref, resid_ref, out_sems = refs
     me = lax.axis_index("dom")
     odd = lax.rem(me, 2)
-    flag = flag_of(basis_ref, 1, gx * gy)
+    flag = flag_of(scale_ref, 1, gx * gy)
     side_cells(gx, gy, remote_ref, odd == 1, disp_ref, flag, side_ref, side_flag_ref, far_force_ref)
     resid = rest_ref[...] - jnp.where(me > 0, far_force_ref[...], 0.0)
-    for ref in resid_refs:
-        ref[...] = resid
-    total = total_ref[...] + project(resid, basis_ref, odd, parts, scaled_ref)
+    resid_ref[...] = resid
+    out_copies = start_copies([resid_ref] * len(resid_hbm), resid_hbm, out_sems)
+    total = total_ref[...] + project(resid, basis_ref, scale_ref, odd, parts, scaled_ref)
     part_ref[...] = total.reshape(part_ref.shape).astype(part_ref.dtype)
+    for copy in out_copies:
+        copy.wait()
 
 
 def fold(value):
@@ -468,38 +502,43 @@
     parts = got_ref.shape[0]
     per = cases // parts
     got = jnp.concatenate([got_ref[source] for source in range(parts)], axis=0)
-    got = jnp.concatenate([got] * (LANES // parts), axis=0).T
-    source = lax.broadcasted_iota(jnp.int32, (LANES, cases), 0)
+    got = jnp.concatenate([got] * per, axis=0).T
+    place = lax.broadcasted_iota(jnp.int32, (owned, LANES), 1) // parts
+    line = jnp.zeros((owned, LANES), F32)
+    for column in range(per):
+        line = jnp.where(place == column, got[column * owned : (column + 1) * owned, :], line)
+    place = lax.broadcasted_iota(jnp.int32, (LANES, cases), 0)
     case = lax.broadcasted_iota(jnp.int32, (LANES, cases), 1)
-    total = None
-    for column in range(per):
-        high, rest = split2(got[column * owned : (column + 1) * owned, :])
-        middle, low = split2(rest)
-        turn = jnp.where((source < parts) & (case == source * per + column), 1.0, 0.0).astype(BF16)
-        for value in (high, middle, low):
-            term = jnp.dot(value.astype(BF16), turn, preferred_element_type=F32)
-            total = term if total is None else total + term
-    out_ref[...] = total
-
-
-def unpermute_kernel(gx, gy, node_ref, near_ref, far_ref, out_ref, parts_ref):
+    turn = jnp.where(case == lax.rem(place, parts) * per + place // parts, 1.0, 0.0).astype(BF16)
+    high, rest = split2(line)
+    middle, low = split2(rest)
+    value = jnp.concatenate([high.astype(BF16), middle.astype(BF16), low.astype(BF16)], axis=0)
+    turned = jnp.dot(value, turn, preferred_element_type=F32)
+    out_ref[...] = turned[:owned] + turned[owned : 2 * owned] + turned[2 * owned :]
+
+
+def unpermute_kernel(gx, gy, node_ref, near_hbm, far_hbm, out_ref, parts_ref, near_ref, far_ref, sems):
     n = gx * gy
     rows, cases = out_ref.shape
-    odd = lax.rem(lax.axis_index("dom"), 2)
-    for ref, layer in ((near_ref, 1 - odd), (far_ref, odd)):
-        high, low = split2(ref[...])
-        parts_ref[rows_of(layer, 3 * n), :cases] = high.astype(BF16)
-        parts_ref[rows_of(layer, 3 * n), cases:] = low.astype(BF16)
+    copies = start_copies((near_hbm, far_hbm), (near_ref, far_ref), sems)
     node = node_ref[...]
     target = jnp.concatenate(
         [3.0 * node[:, layer * n : (layer + 1) * n] + i for layer in range(2) for i in range(3)], axis=1
     ).astype(jnp.int32)
     step = rows // 3
-    for start in range(0, rows, step):
-        here = lax.broadcasted_iota(jnp.int32, (step, rows), 0) + start
-        pick = jnp.where(here == target, 1.0, 0.0).astype(BF16)
+    picks = [
+        jnp.where(lax.broadcasted_iota(jnp.int32, (step, rows), 0) + start == target, 1.0, 0.0).astype(BF16)
+        for start in range(0, rows, step)
+    ]
+    odd = lax.rem(lax.axis_index("dom"), 2)
+    for copy, ref, layer in zip(copies, (near_ref, far_ref), (1 - odd, odd)):
+        copy.wait()
+        high, low = split2(ref[...])
+        parts_ref[rows_of(layer, 3 * n), :cases] = high.astype(BF16)
+        parts_ref[rows_of(layer, 3 * n), cases:] = low.astype(BF16)
+    for i, pick in enumerate(picks):
         both = jnp.dot(pick, parts_ref[...], preferred_element_type=F32)
-        out_ref[start : start + step, :] = both[:, :cases] + both[:, cases:]
+        out_ref[i * step : (i + 1) * step, :] = both[:, :cases] + both[:, cases:]
 
 
 def call(kernel, outs, scratch=(), hbm=(), hbm_out=(), vmem=24, flops=0, nbytes=0):
@@ -546,29 +585,45 @@
     shape = jax.ShapeDtypeStruct
     scratch = pltpu.VMEM
 
+    chips = parts // 2
+    near_pairs = [(d, d ^ 1) for d in range(parts)]
+
     def exchange(value):
         return lax.all_to_all(value, "dom", 0, 0)
+
+    def exchange_chips(value):
+        groups = [list(range(core, parts, 2)) for core in range(2)]
+        return lax.all_to_all(value, "dom", 0, 0, axis_index_groups=groups)
 
     if folded:
         start = exchange(
             call(
-                functools.partial(spread_kernel, parts), shape((parts, owned + SUB, cases), BF16), hbm=(0, 1)
+                functools.partial(spread_kernel, parts),
+                pltpu.HBM((parts, owned + SUB, cases), BF16),
+                [
+                    scratch((parts, owned, cases), BF16),
+                    scratch((parts, SUB, cases), BF16),
+                    pltpu.SemaphoreType.DMA((2,)),
+                ],
+                hbm=(0, 1),
+                hbm_out=(0,),
             )(coef_init, precond.reshape(1, owned))
         )
     else:
         coef = lax.all_gather(coef_init, "dom", axis=0, tiled=True)
         scaling = lax.all_gather(precond, "dom", axis=0, tiled=True)
-    basis_grid, ext_grid, flag_row, nodes = call(
+    basis_grid, scale_grid, ext_grid, flag_row, nodes = call(
         functools.partial(setup_kernel, gx, gy, tile),
         (
-            shape((rows, rank + LANES), BF16),
+            shape((rows, rank), BF16),
+            shape((2, SUB, layer), BF16),
             pltpu.HBM((rows, cases), F32),
             shape((SUB, LANES), F32),
             shape((1, 2 * n), F32),
         ),
-        [scratch((rows, cases), F32), pltpu.SemaphoreType.DMA((1,))],
+        [scratch((rows, cases), F32), pltpu.SemaphoreType.DMA((2,))],
         hbm=(0, 1, 2, 3, 4, 5),
-        hbm_out=(1,),
+        hbm_out=(2,),
         flops=2 * rows * rows * (rank + 2 * cases),
         nbytes=4 * rows * rank,
     )(
@@ -579,23 +634,24 @@
         ext_force,
         basis,
     )
-    near_pairs = [(d, d ^ 1) for d in range(parts)]
     far_pairs = [pair for d in range(1, parts - 1, 2) for pair in ((d, d + 1), (d + 1, d))]
     layer_disp, layer_sent = shape((layer, cases), F32), shape((layer + SUB, cases), BF16)
     side_scratch = [scratch((2 * layer, cases), F32), scratch((n, LANES), F32)]
     columns = shape((SUB, half), F32)
     for sweep in range(ITERS):
         second, last = folded and sweep > 0, sweep == ITERS - 1
-        source = (send if second else start) if folded else coef.astype(BF16)
+        first_source = start if folded else coef.astype(BF16).reshape(parts, owned, cases)
+        source = send if second else (first_source,)
         far_disp, far, coef_rows = call(
-            functools.partial(far_kernel, second),
+            far_kernel if second else functools.partial(first_far_kernel, owned),
             (layer_disp, layer_sent, shape((cases, rank) if second else (rank, cases), BF16)),
+            [scratch((chips, 2, SUB, half), BF16)] if second else (),
             flops=rows * rank * cases,
-        )(source, basis_grid, flag_row)
+        )(*source, basis_grid, scale_grid, flag_row)
         far = lax.ppermute(far, "dom", far_pairs)
         near_disp, near = call(
             functools.partial(near_kernel, second), (layer_disp, layer_sent), flops=rows * rank * cases
-        )(coef_rows, basis_grid, flag_row)
+        )(coef_rows, basis_grid, scale_grid, flag_row)
         near = lax.ppermute(near, "dom", near_pairs)
         prepare = folded and sweep == 0
         disp, force, *mine = call(
@@ -603,33 +659,42 @@
             (shape((rows, cases), F32), shape((rows, cases), F32), *([columns] * 2 if prepare else [])),
             [scratch((n, LANES), F32)],
             flops=rows * rank * cases,
-        )(far_disp, near_disp, basis_grid, *([start] if prepare else []))
+        )(far_disp, near_disp, scale_grid, *([start] if prepare else []))
         if prepare:
             coef_mine, scale_mine = mine
         cut = parts if folded else None
         total_shape = (parts * SUB, half) if folded else (cases, rank)
-        layer_scratch = [*side_scratch, scratch((layer, cases), F32), scratch((layer, cases), BF16)]
+        layer_scratch = [
+            *side_scratch,
+            scratch((layer, cases), F32),
+            scratch((layer, cases), BF16),
+            scratch((layer, cases), F32),
+            pltpu.SemaphoreType.DMA((1,)),
+        ]
         resid_near, rest, total = call(
             functools.partial(side_kernel, gx, gy, cut),
-            (layer_disp, layer_disp, shape(total_shape, F32)),
+            (pltpu.HBM((layer, cases), F32), layer_disp, shape(total_shape, F32)),
             layer_scratch,
-            hbm=(4,),
+            hbm=(5,),
+            hbm_out=(0,),
             flops=rows * rank * cases,
-        )(near, disp, force, basis_grid, ext_grid)
+        )(near, disp, force, basis_grid, scale_grid, ext_grid)
         part_shape = shape((parts, SUB, half), BF16) if folded else shape((cases, rank), F32)
         part, *resid_far = call(
             functools.partial(sweep_kernel, gx, gy, cut),
-            (part_shape, *([layer_disp] if last else [])),
+            (part_shape, *([pltpu.HBM((layer, cases), F32)] if last else [])),
             layer_scratch,
+            hbm_out=(1,) if last else (),
             flops=2 * rows * rank * cases,
-        )(far, disp, rest, total, basis_grid)
+        )(far, disp, rest, total, basis_grid, scale_grid)
         if folded:
             part = exchange(part)
             if not last:
                 coef_mine, send = call(
-                    functools.partial(middle_kernel, rank), (columns, shape(part.shape, BF16))
+                    functools.partial(middle_kernel, rank), (columns, shape((chips, SUB, half), BF16))
                 )(part, coef_mine, scale_mine)
-                send = exchange(send)
+                send = exchange_chips(send)
+                send = send, lax.ppermute(send, "dom", near_pairs)
         else:
             update = scaling[:, None] * lax.psum(part, "dom").T
             root = jnp.sqrt(jnp.sum(update * update, axis=0) / rank + EPSILON)
@@ -638,6 +703,7 @@
         functools.partial(unpermute_kernel, gx, gy),
         shape((rows, cases), F32),
         [scratch((rows, 2 * cases), BF16)],
+        hbm=(1, 2),
         flops=2 * rows * rows * 2 * cases,
     )(nodes, resid_near, resid_far[0])
     if folded:

time: 97.3 us -> 95.7 us (0.984)
  local copies, waits for them, and re-layouts: 2.73 us -> 0 us
  waiting for transfers between devices: 6.16 us -> 8.53 us
    all_to_all x3 -> x2, blocking collectives: 47 us -> 35.6 us  [exchange(): return lax.all_to_all(value, 'dom', 0, 0)]
    all_to_all x0 -> x1, blocking collectives: none -> 11 us  [exchange_chips(): return lax.all_to_all(value, 'dom', 0, 0, axis_index_groups=groups)]
    unnamed x8 -> x0, local copies, waits for them, and re-layouts: 2.73 us -> none
    ppermute x0 -> x1, waiting for transfers between devices: none -> 1.35 us  [on_device(): send = (send, lax.ppermute(send, 'dom', near_pairs))]
    all_to_all x2, waiting for transfers between devices: 6.03 us -> 7.12 us  [exchange(): return lax.all_to_all(value, 'dom', 0, 0)]
  transfers between devices with their start and end apart: 6 -> 7, of which waited for: 3 -> 4; matrix products, arithmetic and copies ran while one was open for 0% -> 0% of each run, Pallas kernels for 19% -> 19%
where the time goes in v1:
time: 95.7 us; the launch traced here: 95.2 us
  blocking collectives  46.6 us (49%)
  Pallas kernels  27.7 us (29%)
  starting transfers between devices  11.5 us (12%)
  waiting for transfers between devices  8.53 us (9%)
    all_to_all x2, blocking collectives, exchange(): return lax.all_to_all(value, 'dom', 0, 0)  35.6 us
    pallas_call x16, Pallas kernels, run(): pl.pallas_call(kernel, out_shape=outs, in_specs=[pl.BlockSpec(memory_spac...  27.7 us
    all_to_all x1, blocking collectives, exchange_chips(): return lax.all_to_all(value, 'dom', 0, 0, axis_index_groups=groups)  11 us
    all_to_all x2, starting transfers between devices, exchange(): return lax.all_to_all(value, 'dom', 0, 0)  9.87 us
    all_to_all x2, waiting for transfers between devices, exchange(): return lax.all_to_all(value, 'dom', 0, 0)  7.12 us
  transfers between devices with their start and end apart: 7, of which 4 were waited for; matrix products, arithmetic and copies ran while one was open for 0% of the time, Pallas kernels for 19%

profile of v1, /device:TPU:0, one launch (start us, length us, event | category | flops | bytes accessed | tf_op | source)
XLA Modules:
  0.0 95.2 jit_solution(14813282985053092843)
XLA Ops:
  0.6 1.6 %shard_map.95 = bf16[32,40,128]{2,1,0:T(8,128)(2,1)} custom-call(f32[32,128]{1,0:T(8,128)} %coef_hbm.1, f32[1,32]{1,0:T(1,128)} %bitcast.5), custom_call_target="tpu_custom_call" | custom-call | tf_op jit(solution)/shard_map/pallas_call | solution.py:556
  2.3 7.3 %all-to-all-start = ((bf16[32,40,128]{2,1,0:T(8,128)(2,1)}), bf16[32,40,128]{2,1,0:T(8,128)(2,1)S(1)}, u32[]{:S(2)}, u32[]{:S(2)}) async-start(bf16[32,40,128]{2,1,0:T(8,128)(2,1)} %shard_map.95), calls=%async_computation | async-start | bytes 655360 | tf_op jit(solution)/shard_map/all_to_all | solution.py:592
  9.6 8.6 %shard_map.96 = (bf16[1536,1024]{1,0:T(8,128)(2,1)S(1)}, bf16[2,8,768]{2,1,0:T(8,128)(2,1)S(1)}, f32[1536,128]{1,0:T(8,128)}, f32[8,128]{1,0:T(8,128)S(1)}, f32[1,512]{1,0:T(1,128)S(1)}) custom-call(s32[1,256]{1,0:T(1,128)} %bitcast.8, f32[1,12]{1,0:T(1,128)} %bitcast.9, s32[8,450]{1,0:T(8,128)} %bitcast.6, s32[1,450]{1,0:T(1,128)} %bitcast.7, ...), custom_call_target="tpu_custom_call" | custom-call | flops 6039797760 | bytes 6291456 | tf_op jit(solution)/shard_map/pallas_call | solution.py:556
  18.2 3.5 %all-to-all-done.source_ref.refs_0_ = bf16[32,40,128]{2,1,0:T(8,128)(2,1)S(1)} async-done(((bf16[32,40,128]{2,1,0:T(8,128)(2,1)}), bf16[32,40,128]{2,1,0:T(8,128)(2,1)S(1)}, u32[]{:S(2)}, u32[]{:S(2)}) %all-to-all-start) | async-done | bytes 327712 | tf_op jit(solution)/shard_map/all_to_all | solution.py:592
  21.6 0.6 shard_map.97
  22.3 0.6 shard_map.98
  23.0 0.7 collective-permute-start
  23.7 0.7 shard_map.99
  24.4 2.5 %shard_map.100 = (f32[768,128]{1,0:T(8,128)}, f32[768,128]{1,0:T(8,128)S(1)}, f32[256,512]{1,0:T(8,128)S(1)}) custom-call(bf16[776,128]{1,0:T(8,128)(2,1)S(1)} %collective-permute-done.1.remote_ref, f32[1536,128]{1,0:T(8,128)S(1)} %get-tuple-element.39.disp_ref, f32[1536,128]{1,0:T(8,128)S(1)} %get-tuple-element.41.force_ref, ...), custom_call_target="tpu_custom_call" | custom-call | flops 201326592 | tf_op jit(solution)/shard_map/pallas_call | solution.py:556
  27.0 1.5 %shard_map.101 = bf16[32,8,512]{2,1,0:T(8,128)(2,1)S(1)} custom-call(bf16[776,128]{1,0:T(8,128)(2,1)S(1)} %collective-permute-done.remote_ref, f32[1536,128]{1,0:T(8,128)S(1)} %get-tuple-element.39.disp_ref, f32[768,128]{1,0:T(8,128)S(1)} %get-tuple-element.43.rest_ref, f32[256,512]{1,0:T(8,128)S(1)} %get-tuple-element.44.total_ref, ...), custom_call_target="tpu_custom_call" | custom-call | flops 402653184 | tf_op jit(solution)/shard_map/pallas_call | solution.py:556
  28.5 17.7 %all_to_all.25.parts_ref = bf16[32,8,512]{2,1,0:T(8,128)(2,1)S(1)} all-to-all(bf16[32,8,512]{2,1,0:T(8,128)(2,1)S(1)} %shard_map.101), channel_id=1, replica_groups=mesh['dom'=32] {'dom'}, dimensions={0} | all-to-all | bytes 524288 | tf_op jit(solution)/shard_map/all_to_all | solution.py:592
  46.4 11.0 %all_to_all.26.same_ref = bf16[16,8,512]{2,1,0:T(8,128)(2,1)S(1)} all-to-all(bf16[16,8,512]{2,1,0:T(8,128)(2,1)S(1)} %get-tuple-element.47), channel_id=1, replica_groups={{0,2,4,6,8,10,12,14,16,18,20,22,24,26,28,30},{1,3,5,7,9,11,13,15,17,19,..., dimensions={0} | all-to-all | bytes 262144 | tf_op jit(solution)/shard_map/all_to_all | solution.py:596
  57.4 1.3 %collective-permute-done.2.other_ref = bf16[16,8,512]{2,1,0:T(8,128)(2,1)S(1)} collective-permute-done((bf16[16,8,512]{2,1,0:T(8,128)(2,1)S(1)}, bf16[16,8,512]{2,1,0:T(8,128)(2,1)S(1)}, u32[]{:S(2)}, u32[]{:S(2)}) %collective-permute-start.2) | collective-permute-done | bytes 131104 | tf_op jit(solution)/shard_map/ppermute | solution.py:697
  58.7 0.8 shard_map.103
  60.4 0.7 collective-permute-start.3
  61.1 0.7 shard_map.105
  61.8 2.5 %shard_map.106 = (f32[768,128]{1,0:T(8,128)}, f32[768,128]{1,0:T(8,128)S(1)}, f32[256,512]{1,0:T(8,128)S(1)}) custom-call(bf16[776,128]{1,0:T(8,128)(2,1)S(1)} %collective-permute-done.4.remote_ref, f32[1536,128]{1,0:T(8,128)S(1)} %get-tuple-element.52.disp_ref, f32[1536,128]{1,0:T(8,128)S(1)} %get-tuple-element.54.force_ref, ...), custom_call_target="tpu_custom_call" | custom-call | flops 201326592 | tf_op jit(solution)/shard_map/pallas_call | solution.py:556
  64.3 1.5 %shard_map.107 = (bf16[32,8,512]{2,1,0:T(8,128)(2,1)S(1)}, f32[768,128]{1,0:T(8,128)}) custom-call(bf16[776,128]{1,0:T(8,128)(2,1)S(1)} %collective-permute-done.3.remote_ref, f32[1536,128]{1,0:T(8,128)S(1)} %get-tuple-element.52.disp_ref, f32[768,128]{1,0:T(8,128)S(1)} %get-tuple-element.55.rest_ref, f32[256,512]{1,0:T(8,128)S(1)} %get-tuple-element.56.total_ref, ...), custom_call_target="tpu_custom_call" | custom-call | flops 402653184 | tf_op jit(solution)/shard_map/pallas_call | solution.py:556
  65.8 17.9 %all_to_all.27.parts_ref = bf16[32,8,512]{2,1,0:T(8,128)(2,1)S(1)} all-to-all(bf16[32,8,512]{2,1,0:T(8,128)(2,1)S(1)} %get-tuple-element.57), channel_id=1, replica_groups=mesh['dom'=32] {'dom'}, dimensions={0} | all-to-all | bytes 524288 | tf_op jit(solution)/shard_map/all_to_all | solution.py:592
  83.8 0.9 shard_map.108
  84.7 2.5 %all-to-all-start.4 = ((f32[32,1,128]{2,1,0:T(1,128)}), f32[32,1,128]{2,1,0:T(1,128)S(1)}, u32[]{:S(2)}, u32[]{:S(2)}) async-start(f32[32,1,128]{2,1,0:T(1,128)} %shard_map.108), calls=%async_computation.4 | async-start | bytes 32768 | tf_op jit(solution)/shard_map/all_to_all | solution.py:592
  87.3 3.5 %shard_map.110 = f32[1536,128]{1,0:T(8,128)} custom-call(f32[1,512]{1,0:T(1,128)S(1)} %get-tuple-element.59.node_ref, f32[768,128]{1,0:T(8,128)} %get-tuple-element.60.near_hbm, f32[768,128]{1,0:T(8,128)} %get-tuple-element.61.far_hbm), custom_call_target="tpu_custom_call" | custom-call | flops 1207959552 | tf_op jit(solution)/shard_map/pallas_call | solution.py:556
  90.7 3.6 %all-to-all-done.4.got_ref = f32[32,1,128]{2,1,0:T(1,128)S(1)} async-done(((f32[32,1,128]{2,1,0:T(1,128)}), f32[32,1,128]{2,1,0:T(1,128)S(1)}, u32[]{:S(2)}, u32[]{:S(2)}) %all-to-all-start.4) | async-done | bytes 16416 | tf_op jit(solution)/shard_map/all_to_all | solution.py:592
  94.4 0.8 shard_map.109
  (9 shorter events, 1.2 us)
Async XLA Ops:
  2.3 19.4 %all-to-all-start = ((bf16[32,40,128]{2,1,0:T(8,128)(2,1)}), bf16[32,40,128]{2,1,0:T(8,128)(2,1)S(1)}, u32[]{:S(2)}, u32[]{:S(2)}) async-start(bf16[32,40,128]{2,1,0:T(8,128)(2,1)} %shard_map.95), calls=%async_computation | async-start | bytes 655360 | tf_op jit(solution)/shard_map/all_to_all | solution.py:592
  22.9 1.5 %collective-permute-start.1 = (bf16[776,128]{1,0:T(8,128)(2,1)S(1)}, bf16[776,128]{1,0:T(8,128)(2,1)S(1)}, u32[]{:S(2)}, u32[]{:S(2)}) collective-permute-start(bf16[776,128]{1,0:T(8,128)(2,1)S(1)} %get-tuple-element.40), channel_id=1, source_target_pairs={{0,1},{1,0},{2,3},{3,2},{4,5},{5,4},{6,7},{7,6},{8,9},{9,8},{10,11... | collective-permute-start | bytes 595976 | tf_op jit(solution)/shard_map/ppermute | solution.py:655
  23.0 4.0 %collective-permute-start = (bf16[776,128]{1,0:T(8,128)(2,1)S(1)}, bf16[776,128]{1,0:T(8,128)(2,1)S(1)}, u32[]{:S(2)}, u32[]{:S(2)}) collective-permute-start(bf16[776,128]{1,0:T(8,128)(2,1)S(1)} %get-tuple-element.35), channel_id=1, source_target_pairs={{1,2},{2,1},{3,4},{4,3},{5,6},{6,5},{7,8},{8,7},{9,10},{10,9},{11,... | collective-permute-start | bytes 595976 | tf_op jit(solution)/shard_map/ppermute | solution.py:651
  57.4 1.3 %collective-permute-start.2 = (bf16[16,8,512]{2,1,0:T(8,128)(2,1)S(1)}, bf16[16,8,512]{2,1,0:T(8,128)(2,1)S(1)}, u32[]{:S(2)}, u32[]{:S(2)}) collective-permute-start(bf16[16,8,512]{2,1,0:T(8,128)(2,1)S(1)} %all_to_all.26.same_ref), channel_id=1, source_target_pairs={{0,1},{1,0},{2,3},{3,2},{4,5},{5,4},{6,7},{7,6},{8,9},{9,8},{10,11... | collective-permute-start | bytes 393224 | tf_op jit(solution)/shard_map/ppermute | solution.py:697
  60.2 1.6 %collective-permute-start.4 = (bf16[776,128]{1,0:T(8,128)(2,1)S(1)}, bf16[776,128]{1,0:T(8,128)(2,1)S(1)}, u32[]{:S(2)}, u32[]{:S(2)}) collective-permute-start(bf16[776,128]{1,0:T(8,128)(2,1)S(1)} %get-tuple-element.53), channel_id=1, source_target_pairs={{0,1},{1,0},{2,3},{3,2},{4,5},{5,4},{6,7},{7,6},{8,9},{9,8},{10,11... | collective-permute-start | bytes 595976 | tf_op jit(solution)/shard_map/ppermute | solution.py:655
  60.4 3.9 %collective-permute-start.3 = (bf16[776,128]{1,0:T(8,128)(2,1)S(1)}, bf16[776,128]{1,0:T(8,128)(2,1)S(1)}, u32[]{:S(2)}, u32[]{:S(2)}) collective-permute-start(bf16[776,128]{1,0:T(8,128)(2,1)S(1)} %get-tuple-element.48), channel_id=1, source_target_pairs={{1,2},{2,1},{3,4},{4,3},{5,6},{6,5},{7,8},{8,7},{9,10},{10,9},{11,... | collective-permute-start | bytes 595976 | tf_op jit(solution)/shard_map/ppermute | solution.py:651
  84.7 9.7 %all-to-all-start.4 = ((f32[32,1,128]{2,1,0:T(1,128)}), f32[32,1,128]{2,1,0:T(1,128)S(1)}, u32[]{:S(2)}, u32[]{:S(2)}) async-start(f32[32,1,128]{2,1,0:T(1,128)} %shard_map.108), calls=%async_computation.4 | async-start | bytes 32768 | tf_op jit(solution)/shard_map/all_to_all | solution.py:592

commit v2 on v1

--- a/solution.py
+++ b/solution.py
@@ -133,10 +133,10 @@
 def setup_kernel(
     gx, gy, tile, halo_hbm, scale_hbm, conn_hbm, plastic_hbm, ext_hbm, basis_hbm,
     out_ref, scale_out_ref, ext_out, flag_row_ref, node_ref,
-    ext_grid_ref, out_sems, halo_ref, scale_ref, conn_ref, plastic_ref, ext_ref, basis_ref, sems,
+    ext_grid_ref, pick_ref, out_sems, halo_ref, scale_ref, conn_ref, plastic_ref, ext_ref, basis_ref, sems,
 ):
     n = gx * gy
-    rows, _ = basis_ref.shape
+    rows, rank = basis_ref.shape
     copies = start_copies(
         (halo_hbm, scale_hbm, conn_hbm, plastic_hbm, ext_hbm, basis_hbm),
         (halo_ref, scale_ref, conn_ref, plastic_ref, ext_ref, basis_ref),
@@ -168,26 +168,21 @@
     high, low = split2(ext_ref[...])
     cases = ext_ref.shape[1]
     loads = jnp.concatenate([high.astype(BF16), low.astype(BF16)], axis=1)
-    copies[5].wait()
-    out_copies = []
     for layer, node in enumerate((node0, node1)):
         for i in range(3):
             start = (3 * layer + i) * n
-            pick = select_rows(node, i, rows)
-            both = jnp.dot(pick, loads, preferred_element_type=F32)
-            ext_grid_ref[start : start + n, :] = both[:, :cases] + both[:, cases:]
-            if i == 2:
-                done = slice(3 * n * layer, 3 * n * (layer + 1))
-                out_copies.append(
-                    pltpu.make_async_copy(ext_grid_ref.at[done, :], ext_out.at[done, :], out_sems.at[layer])
-                )
-                out_copies[-1].start()
+            pick_ref[start : start + n, :] = select_rows(node, i, rows)
             scale_out_ref[layer, :, i * n : (i + 1) * n] = scale_block(
                 node_rows[layer], i, scale_col, tile, flag_rows[layer]
             )
-            out_ref[start : start + n, :] = jnp.dot(
-                pick, basis_ref[...], preferred_element_type=F32
-            ).astype(BF16)
+    both = jnp.dot(pick_ref[...], loads, preferred_element_type=F32)
+    ext_grid_ref[...] = both[:, :cases] + both[:, cases:]
+    out_copies = start_copies((ext_grid_ref,), (ext_out,), out_sems)
+    copies[5].wait()
+    for part in range(0, rank, 256):
+        out_ref[:, part : part + 256] = jnp.dot(
+            pick_ref[...], basis_ref[:, part : part + 256], preferred_element_type=F32
+        ).astype(BF16)
     for copy in out_copies:
         copy.wait()
 
@@ -621,7 +616,7 @@
             shape((SUB, LANES), F32),
             shape((1, 2 * n), F32),
         ),
-        [scratch((rows, cases), F32), pltpu.SemaphoreType.DMA((2,))],
+        [scratch((rows, cases), F32), scratch((rows, rows), BF16), pltpu.SemaphoreType.DMA((1,))],
         hbm=(0, 1, 2, 3, 4, 5),
         hbm_out=(2,),
         flops=2 * rows * rows * (rank + 2 * cases),

time: 95.7 us -> 95.7 us (level)
  no operation moved by 1% of the time
where the time goes in v2:
time: 95.7 us; the launch traced here: 95.2 us
  blocking collectives  46.6 us (49%)
  Pallas kernels  27.1 us (28%)
  starting transfers between devices  11.5 us (12%)
  waiting for transfers between devices  9.19 us (10%)
    all_to_all x2, blocking collectives, exchange(): return lax.all_to_all(value, 'dom', 0, 0)  35.6 us
    pallas_call x16, Pallas kernels, run(): pl.pallas_call(kernel, out_shape=outs, in_specs=[pl.BlockSpec(memory_spac...  27.1 us
    all_to_all x1, blocking collectives, exchange_chips(): return lax.all_to_all(value, 'dom', 0, 0, axis_index_groups=groups)  11 us
    all_to_all x2, starting transfers between devices, exchange(): return lax.all_to_all(value, 'dom', 0, 0)  9.87 us
    all_to_all x2, waiting for transfers between devices, exchange(): return lax.all_to_all(value, 'dom', 0, 0)  7.78 us
  transfers between devices with their start and end apart: 7, of which 4 were waited for; matrix products, arithmetic and copies ran while one was open for 0% of the time, Pallas kernels for 19%

profile of v2, /device:TPU:0, one launch (start us, length us, event | category | flops | bytes accessed | tf_op | source)
XLA Modules:
  0.0 95.2 jit_solution(15651578694345117736)
XLA Ops:
  0.6 1.6 %shard_map.95 = bf16[32,40,128]{2,1,0:T(8,128)(2,1)} custom-call(f32[32,128]{1,0:T(8,128)} %coef_hbm.1, f32[1,32]{1,0:T(1,128)} %bitcast.5), custom_call_target="tpu_custom_call" | custom-call | tf_op jit(solution)/shard_map/pallas_call | solution.py:551
  2.3 7.3 %all-to-all-start = ((bf16[32,40,128]{2,1,0:T(8,128)(2,1)}), bf16[32,40,128]{2,1,0:T(8,128)(2,1)S(1)}, u32[]{:S(2)}, u32[]{:S(2)}) async-start(bf16[32,40,128]{2,1,0:T(8,128)(2,1)} %shard_map.95), calls=%async_computation | async-start | bytes 655360 | tf_op jit(solution)/shard_map/all_to_all | solution.py:587
  9.6 7.9 %shard_map.96 = (bf16[1536,1024]{1,0:T(8,128)(2,1)S(1)}, bf16[2,8,768]{2,1,0:T(8,128)(2,1)S(1)}, f32[1536,128]{1,0:T(8,128)}, f32[8,128]{1,0:T(8,128)S(1)}, f32[1,512]{1,0:T(1,128)S(1)}) custom-call(s32[1,256]{1,0:T(1,128)} %bitcast.8, f32[1,12]{1,0:T(1,128)} %bitcast.9, s32[8,450]{1,0:T(8,128)} %bitcast.6, s32[1,450]{1,0:T(1,128)} %bitcast.7, ...), custom_call_target="tpu_custom_call" | custom-call | flops 6039797760 | bytes 6291456 | tf_op jit(solution)/shard_map/pallas_call | solution.py:551
  17.5 4.1 %all-to-all-done.source_ref.refs_0_ = bf16[32,40,128]{2,1,0:T(8,128)(2,1)S(1)} async-done(((bf16[32,40,128]{2,1,0:T(8,128)(2,1)}), bf16[32,40,128]{2,1,0:T(8,128)(2,1)S(1)}, u32[]{:S(2)}, u32[]{:S(2)}) %all-to-all-start) | async-done | bytes 327712 | tf_op jit(solution)/shard_map/all_to_all | solution.py:587
  21.6 0.6 shard_map.97
  22.3 0.6 shard_map.98
  23.0 0.7 collective-permute-start
  23.7 0.7 shard_map.99
  24.4 2.5 %shard_map.100 = (f32[768,128]{1,0:T(8,128)}, f32[768,128]{1,0:T(8,128)S(1)}, f32[256,512]{1,0:T(8,128)S(1)}) custom-call(bf16[776,128]{1,0:T(8,128)(2,1)S(1)} %collective-permute-done.1.remote_ref, f32[1536,128]{1,0:T(8,128)S(1)} %get-tuple-element.39.disp_ref, f32[1536,128]{1,0:T(8,128)S(1)} %get-tuple-element.41.force_ref, ...), custom_call_target="tpu_custom_call" | custom-call | flops 201326592 | tf_op jit(solution)/shard_map/pallas_call | solution.py:551
  27.0 1.5 %shard_map.101 = bf16[32,8,512]{2,1,0:T(8,128)(2,1)S(1)} custom-call(bf16[776,128]{1,0:T(8,128)(2,1)S(1)} %collective-permute-done.remote_ref, f32[1536,128]{1,0:T(8,128)S(1)} %get-tuple-element.39.disp_ref, f32[768,128]{1,0:T(8,128)S(1)} %get-tuple-element.43.rest_ref, f32[256,512]{1,0:T(8,128)S(1)} %get-tuple-element.44.total_ref, ...), custom_call_target="tpu_custom_call" | custom-call | flops 402653184 | tf_op jit(solution)/shard_map/pallas_call | solution.py:551
  28.5 17.7 %all_to_all.25.parts_ref = bf16[32,8,512]{2,1,0:T(8,128)(2,1)S(1)} all-to-all(bf16[32,8,512]{2,1,0:T(8,128)(2,1)S(1)} %shard_map.101), channel_id=1, replica_groups=mesh['dom'=32] {'dom'}, dimensions={0} | all-to-all | bytes 524288 | tf_op jit(solution)/shard_map/all_to_all | solution.py:587
  46.4 11.0 %all_to_all.26.same_ref = bf16[16,8,512]{2,1,0:T(8,128)(2,1)S(1)} all-to-all(bf16[16,8,512]{2,1,0:T(8,128)(2,1)S(1)} %get-tuple-element.47), channel_id=1, replica_groups={{0,2,4,6,8,10,12,14,16,18,20,22,24,26,28,30},{1,3,5,7,9,11,13,15,17,19,..., dimensions={0} | all-to-all | bytes 262144 | tf_op jit(solution)/shard_map/all_to_all | solution.py:591
  57.4 1.3 %collective-permute-done.2.other_ref = bf16[16,8,512]{2,1,0:T(8,128)(2,1)S(1)} collective-permute-done((bf16[16,8,512]{2,1,0:T(8,128)(2,1)S(1)}, bf16[16,8,512]{2,1,0:T(8,128)(2,1)S(1)}, u32[]{:S(2)}, u32[]{:S(2)}) %collective-permute-start.2) | collective-permute-done | bytes 131104 | tf_op jit(solution)/shard_map/ppermute | solution.py:692
  58.7 0.8 shard_map.103
  60.4 0.7 collective-permute-start.3
  61.1 0.7 shard_map.105
  61.8 2.5 %shard_map.106 = (f32[768,128]{1,0:T(8,128)}, f32[768,128]{1,0:T(8,128)S(1)}, f32[256,512]{1,0:T(8,128)S(1)}) custom-call(bf16[776,128]{1,0:T(8,128)(2,1)S(1)} %collective-permute-done.4.remote_ref, f32[1536,128]{1,0:T(8,128)S(1)} %get-tuple-element.52.disp_ref, f32[1536,128]{1,0:T(8,128)S(1)} %get-tuple-element.54.force_ref, ...), custom_call_target="tpu_custom_call" | custom-call | flops 201326592 | tf_op jit(solution)/shard_map/pallas_call | solution.py:551
  64.3 1.5 %shard_map.107 = (bf16[32,8,512]{2,1,0:T(8,128)(2,1)S(1)}, f32[768,128]{1,0:T(8,128)}) custom-call(bf16[776,128]{1,0:T(8,128)(2,1)S(1)} %collective-permute-done.3.remote_ref, f32[1536,128]{1,0:T(8,128)S(1)} %get-tuple-element.52.disp_ref, f32[768,128]{1,0:T(8,128)S(1)} %get-tuple-element.55.rest_ref, f32[256,512]{1,0:T(8,128)S(1)} %get-tuple-element.56.total_ref, ...), custom_call_target="tpu_custom_call" | custom-call | flops 402653184 | tf_op jit(solution)/shard_map/pallas_call | solution.py:551
  65.8 17.9 %all_to_all.27.parts_ref = bf16[32,8,512]{2,1,0:T(8,128)(2,1)S(1)} all-to-all(bf16[32,8,512]{2,1,0:T(8,128)(2,1)S(1)} %get-tuple-element.57), channel_id=1, replica_groups=mesh['dom'=32] {'dom'}, dimensions={0} | all-to-all | bytes 524288 | tf_op jit(solution)/shard_map/all_to_all | solution.py:587
  83.8 0.9 shard_map.108
  84.7 2.5 %all-to-all-start.4 = ((f32[32,1,128]{2,1,0:T(1,128)}), f32[32,1,128]{2,1,0:T(1,128)S(1)}, u32[]{:S(2)}, u32[]{:S(2)}) async-start(f32[32,1,128]{2,1,0:T(1,128)} %shard_map.108), calls=%async_computation.4 | async-start | bytes 32768 | tf_op jit(solution)/shard_map/all_to_all | solution.py:587
  87.3 3.5 %shard_map.110 = f32[1536,128]{1,0:T(8,128)} custom-call(f32[1,512]{1,0:T(1,128)S(1)} %get-tuple-element.59.node_ref, f32[768,128]{1,0:T(8,128)} %get-tuple-element.60.near_hbm, f32[768,128]{1,0:T(8,128)} %get-tuple-element.61.far_hbm), custom_call_target="tpu_custom_call" | custom-call | flops 1207959552 | tf_op jit(solution)/shard_map/pallas_call | solution.py:551
  90.7 3.6 %all-to-all-done.4.got_ref = f32[32,1,128]{2,1,0:T(1,128)S(1)} async-done(((f32[32,1,128]{2,1,0:T(1,128)}), f32[32,1,128]{2,1,0:T(1,128)S(1)}, u32[]{:S(2)}, u32[]{:S(2)}) %all-to-all-start.4) | async-done | bytes 16416 | tf_op jit(solution)/shard_map/all_to_all | solution.py:587
  94.4 0.8 shard_map.109
  (9 shorter events, 1.2 us)
Async XLA Ops:
  2.3 19.4 %all-to-all-start = ((bf16[32,40,128]{2,1,0:T(8,128)(2,1)}), bf16[32,40,128]{2,1,0:T(8,128)(2,1)S(1)}, u32[]{:S(2)}, u32[]{:S(2)}) async-start(bf16[32,40,128]{2,1,0:T(8,128)(2,1)} %shard_map.95), calls=%async_computation | async-start | bytes 655360 | tf_op jit(solution)/shard_map/all_to_all | solution.py:587
  22.9 1.5 %collective-permute-start.1 = (bf16[776,128]{1,0:T(8,128)(2,1)S(1)}, bf16[776,128]{1,0:T(8,128)(2,1)S(1)}, u32[]{:S(2)}, u32[]{:S(2)}) collective-permute-start(bf16[776,128]{1,0:T(8,128)(2,1)S(1)} %get-tuple-element.40), channel_id=1, source_target_pairs={{0,1},{1,0},{2,3},{3,2},{4,5},{5,4},{6,7},{7,6},{8,9},{9,8},{10,11... | collective-permute-start | bytes 595976 | tf_op jit(solution)/shard_map/ppermute | solution.py:650
  23.0 4.0 %collective-permute-start = (bf16[776,128]{1,0:T(8,128)(2,1)S(1)}, bf16[776,128]{1,0:T(8,128)(2,1)S(1)}, u32[]{:S(2)}, u32[]{:S(2)}) collective-permute-start(bf16[776,128]{1,0:T(8,128)(2,1)S(1)} %get-tuple-element.35), channel_id=1, source_target_pairs={{1,2},{2,1},{3,4},{4,3},{5,6},{6,5},{7,8},{8,7},{9,10},{10,9},{11,... | collective-permute-start | bytes 595976 | tf_op jit(solution)/shard_map/ppermute | solution.py:646
  57.4 1.3 %collective-permute-start.2 = (bf16[16,8,512]{2,1,0:T(8,128)(2,1)S(1)}, bf16[16,8,512]{2,1,0:T(8,128)(2,1)S(1)}, u32[]{:S(2)}, u32[]{:S(2)}) collective-permute-start(bf16[16,8,512]{2,1,0:T(8,128)(2,1)S(1)} %all_to_all.26.same_ref), channel_id=1, source_target_pairs={{0,1},{1,0},{2,3},{3,2},{4,5},{5,4},{6,7},{7,6},{8,9},{9,8},{10,11... | collective-permute-start | bytes 393224 | tf_op jit(solution)/shard_map/ppermute | solution.py:692
  60.2 1.6 %collective-permute-start.4 = (bf16[776,128]{1,0:T(8,128)(2,1)S(1)}, bf16[776,128]{1,0:T(8,128)(2,1)S(1)}, u32[]{:S(2)}, u32[]{:S(2)}) collective-permute-start(bf16[776,128]{1,0:T(8,128)(2,1)S(1)} %get-tuple-element.53), channel_id=1, source_target_pairs={{0,1},{1,0},{2,3},{3,2},{4,5},{5,4},{6,7},{7,6},{8,9},{9,8},{10,11... | collective-permute-start | bytes 595976 | tf_op jit(solution)/shard_map/ppermute | solution.py:650
  60.4 3.9 %collective-permute-start.3 = (bf16[776,128]{1,0:T(8,128)(2,1)S(1)}, bf16[776,128]{1,0:T(8,128)(2,1)S(1)}, u32[]{:S(2)}, u32[]{:S(2)}) collective-permute-start(bf16[776,128]{1,0:T(8,128)(2,1)S(1)} %get-tuple-element.48), channel_id=1, source_target_pairs={{1,2},{2,1},{3,4},{4,3},{5,6},{6,5},{7,8},{8,7},{9,10},{10,9},{11,... | collective-permute-start | bytes 595976 | tf_op jit(solution)/shard_map/ppermute | solution.py:646
  84.7 9.7 %all-to-all-start.4 = ((f32[32,1,128]{2,1,0:T(1,128)}), f32[32,1,128]{2,1,0:T(1,128)S(1)}, u32[]{:S(2)}, u32[]{:S(2)}) async-start(f32[32,1,128]{2,1,0:T(1,128)} %shard_map.108), calls=%async_computation.4 | async-start | bytes 32768 | tf_op jit(solution)/shard_map/all_to_all | solution.py:587
